TPU v7x, 256 devices: a whole 4x4x8 slice. The times are simulated.
256 devices in a mesh: blk: 32 (over z, x_lo, core), head: 8 (over x_hi, y).
Axes of the slice: x: 4 (x_hi: 2, x_lo: 2; x = x_hi * 2 + x_lo), y: 4, z: 8, core: 2. Of those that a mesh axis runs over, the one named last changes fastest.
Arguments:
- query_tokens: bfloat16 [16384, 3072], P(('blk', 'head')), may hold values from -12 to 12
- key_tokens: bfloat16 [16384, 3072], P(('blk', 'head')), may hold values from -6 to 6
- value_tokens: bfloat16 [16384, 3072], P(('blk', 'head')), may hold values from -6 to 6
- out_weight: bfloat16 [3072, 3072], P('head'), may hold values from -1.75 to 1.75
- kv_blocks: int32 [128, 16], P('blk'), may hold values from -1 to 127, as said below
Outputs:
- projected: bfloat16 [16384, 3072], P(('blk', 'head'))
Inputs may be any that keep to these rules, and one draw needn't show every extreme that they name: `kv_blocks`: row i lists the key blocks of 128 tokens that query block i attends to; let G = floor(i / 4). Entry 0 is i. Entry 1 is one of the blocks 4 * M to 4 * M + 3 with M = (G + 16) mod 32. Entry j >= 2 is -1 (absent) or one of the blocks 4 * (G + o) to 4 * (G + o) + 3, with o = j // 2 for even j and o = -(j - 1) // 2 for odd j; it is present whenever j < 8 and those blocks exist. Entries of one row are distinct.
All inputs are finite; a program needn't handle non-finite values.
Results may differ from a plain program's by a relative error of at most 0.012.
Values may be sent and summed in bfloat16 or wider, within the bound.
A program may use at most 128 MiB of HBM per device.

v0:
```python
import math

import jax
import jax.numpy as jnp
from jax import lax
from jax.sharding import PartitionSpec as P

HD = 128


masked_low = -1e30


def sparse_attend(query_sets, key_sets, value_sets, present):
    blocks_dev = present.shape[0]
    slots = present.shape[1]
    block_rows = query_sets.shape[2]
    scaling = 1.0 / math.sqrt(HD)
    allowed = jnp.broadcast_to(present[:, :, None], (blocks_dev, slots, block_rows)).reshape(
        blocks_dev, slots * block_rows
    )
    scores = (
        jnp.einsum("hbqd,hbkd->hbqk", query_sets, key_sets, preferred_element_type=jnp.float32)
        * scaling
    )
    mask_full = allowed[None, :, None, :]
    peak_value = jnp.max(jnp.where(mask_full, scores, masked_low), axis=-1, keepdims=True)
    weights = jnp.where(mask_full, jnp.exp(scores - peak_value), 0.0)
    denom = jnp.sum(weights, axis=-1)
    outputs = jnp.einsum(
        "hbqk,hbkd->hbqd",
        weights.astype(jnp.bfloat16),
        value_sets,
        preferred_element_type=jnp.float32,
    )
    return outputs / denom[..., None]


def on_device(query_tokens, key_tokens, value_tokens, out_weight, kv_blocks):
    queries, key_rows, value_rows = (
        lax.all_to_all(query_tokens, "head", split_axis=1, concat_axis=0, tiled=True),
        lax.all_to_all(key_tokens, "head", split_axis=1, concat_axis=0, tiled=True),
        lax.all_to_all(value_tokens, "head", split_axis=1, concat_axis=0, tiled=True),
    )
    row_total = queries.shape[0]
    feature_width = queries.shape[1]
    heads_dev = feature_width // HD
    blocks_dev = kv_blocks.shape[0]
    block_rows = row_total // blocks_dev
    slots = kv_blocks.shape[1]
    query_heads = queries.reshape(row_total, heads_dev, HD).transpose(1, 0, 2)
    query_sets = query_heads.reshape(heads_dev, blocks_dev, block_rows, HD)
    key_heads = key_rows.reshape(row_total, heads_dev, HD).transpose(1, 0, 2)
    value_heads = value_rows.reshape(row_total, heads_dev, HD).transpose(1, 0, 2)
    present = kv_blocks >= 0
    safe_index = jnp.maximum(kv_blocks, 0)
    gathered_keys, gathered_values = (
        lax.all_gather(key_heads, "blk", axis=1, tiled=True),
        lax.all_gather(value_heads, "blk", axis=1, tiled=True),
    )
    total_blocks = gathered_keys.shape[1] // block_rows
    source_keys = gathered_keys.reshape(heads_dev, total_blocks, block_rows, HD)
    source_values = gathered_values.reshape(heads_dev, total_blocks, block_rows, HD)
    flat_index = safe_index.reshape(blocks_dev * slots)
    key_sets = jnp.take(source_keys, flat_index, axis=1).reshape(
        heads_dev, blocks_dev, slots * block_rows, HD
    )
    value_sets = jnp.take(source_values, flat_index, axis=1).reshape(
        heads_dev, blocks_dev, slots * block_rows, HD
    )
    outputs = sparse_attend(query_sets, key_sets, value_sets, present)
    attended = (
        outputs.reshape(heads_dev, row_total, HD)
        .transpose(1, 0, 2)
        .reshape(row_total, feature_width)
    )
    attended = attended.astype(jnp.bfloat16)
    return lax.psum_scatter(
        jnp.dot(attended, out_weight, preferred_element_type=jnp.float32).astype(jnp.bfloat16),
        "head",
        scatter_dimension=0,
        tiled=True,
    )


def solution(mesh):
    placed = (
        P(("blk", "head"), None),
        P(("blk", "head"), None),
        P(("blk", "head"), None),
        P("head", None),
        P("blk", None),
    )
    return jax.shard_map(
        on_device, mesh=mesh, in_specs=placed, out_specs=P(("blk", "head"), None), check_vma=False
    )
```

profile of v0, /device:TPU:8, one launch (start us, length us, event | category | flops | bytes accessed | tf_op | source)
XLA Modules:
  0.0 321.5 jit_solution(16858350131159604797)
XLA Ops:
  6.5 0.0 copy-start
  6.5 0.0 copy-start.1
  6.5 0.0 all-gather.3.cloned.1.call-start
  6.5 1.2 copy.46
  7.7 15.8 %all_to_all.48 = bf16[64,8,384]{2,0,1:T(8,128)(2,1)S(1)} all-to-all(bf16[64,8,384]{2,0,1:T(8,128)(2,1)S(1)} %bitcast.64), channel_id=1, replica_groups=mesh['blk'=32,'head'=8] {'head'}, dimensions={1} | all-to-all | bytes 786432 | tf_op jit(solution)/shard_map/all_to_all | solution.py:42
  23.6 0.1 reshape.52
  23.7 0.8 copy.26
  24.5 0.0 all-gather.3.cloned.1.call-update
  24.5 0.0 all-gather.5.cloned.1.call-start
  24.6 1.0 copy.44
  25.6 12.0 %all_to_all.49 = bf16[64,8,384]{2,0,1:T(8,128)(2,1)S(1)} all-to-all(bf16[64,8,384]{2,0,1:T(8,128)(2,1)S(1)} %bitcast.65), channel_id=1, replica_groups=mesh['blk'=32,'head'=8] {'head'}, dimensions={1} | all-to-all | bytes 786432 | tf_op jit(solution)/shard_map/all_to_all | solution.py:43
  37.6 0.1 reshape.58
  37.8 0.8 copy.31
  38.6 0.0 all-gather.5.cloned.1.call-update
  38.6 1.8 copy.45
  40.5 4.9 %all-to-all-start.1 = ((bf16[64,8,384]{2,0,1:T(8,128)(2,1)}), bf16[64,8,384]{2,0,1:T(8,128)(2,1)S(1)}, u32[]{:S(2)}, u32[]{:S(2)}) async-start(bf16[64,8,384]{2,0,1:T(8,128)(2,1)} %bitcast.51), calls=%async_computation.1 | async-start | bytes 786432 | tf_op jit(solution)/shard_map/all_to_all | solution.py:41
  45.3 0.0 reduce-scatter.2.cloned.1.call-start
  45.3 0.0 copy-done.1
  45.4 0.1 reshape.54
  45.4 0.1 broadcast_bitcast_fusion
  45.6 11.7 %all-to-all-done.1 = bf16[64,8,384]{2,0,1:T(8,128)(2,1)S(1)} async-done(((bf16[64,8,384]{2,0,1:T(8,128)(2,1)}), bf16[64,8,384]{2,0,1:T(8,128)(2,1)S(1)}, u32[]{:S(2)}, u32[]{:S(2)}) %all-to-all-start.1) | async-done | bytes 393248 | tf_op jit(solution)/shard_map/all_to_all | solution.py:41
  57.2 0.1 reshape.56
  57.3 0.1 copy.29
  57.4 49.7 %all-gather.3.cloned.1.call-done = bf16[3,16384,128]{2,1,0:T(8,128)(2,1)} async-done(((bf16[3,512,128]{2,1,0:T(8,128)(2,1)}), bf16[3,16384,128]{2,1,0:T(8,128)(2,1)}) %all-gather.3.cloned.1.call-update) | async-done | bytes 12582928 | tf_op jit(solution)/shard_map/all_gather | solution.py:58
  107.2 8.6 %gather_fusion = bf16[64,3,128,128]{3,2,1,0:T(8,128)(2,1)} fusion(bf16[3,128,128,128]{3,2,1,0:T(8,128)(2,1)} %bitcast.56, s32[1024]{0:T(1024)S(1)} %pad_clamp_fusion), kind=kCustom, calls=%fused_computation.clone | custom fusion | bytes 12583168 | tf_op jit(solution)/shard_map/jit(_take)/gather | solution.py:65
  115.8 72.1 %all-gather.5.cloned.1.call-done = bf16[3,16384,128]{2,1,0:T(8,128)(2,1)} async-done(((bf16[3,512,128]{2,1,0:T(8,128)(2,1)}), bf16[3,16384,128]{2,1,0:T(8,128)(2,1)}) %all-gather.5.cloned.1.call-update) | async-done | bytes 12582928 | tf_op jit(solution)/shard_map/all_gather | solution.py:59
  187.9 8.5 %gather_fusion.1 = bf16[64,3,128,128]{3,2,1,0:T(8,128)(2,1)} fusion(bf16[3,128,128,128]{3,2,1,0:T(8,128)(2,1)} %bitcast.57, s32[1024]{0:T(1024)S(1)} %pad_clamp_fusion), kind=kCustom, calls=%fused_computation.1.clone | custom fusion | bytes 12583168 | tf_op jit(solution)/shard_map/jit(_take)/gather | solution.py:68
  196.4 5.5 %select_bitcast_fusion.1 = (bf16[3,64,128,128]{3,2,0,1:T(8,128)(2,1)S(1)}, bf16[3,64,128,128]{3,2,0,1:T(8,128)(2,1)S(1)}) fusion(bf16[64,3,128,128]{3,2,1,0:T(8,128)(2,1)} %gather_fusion, pred[64]{0:T(512)(128)(4,1)S(1)} %compare_and_fusion, bf16[64,3,128,128]{3,2,1,0:T(8,128)(2,1)} %gather_fusion.1), kind=kLoop, calls=%fused_computation.11 | loop fusion | flops 6291456 | bytes 25165888 | tf_op jit(solution)/shard_map/jit(_take)/select_n | solution.py:65
  202.0 4.0 %copy.27 = bf16[3,64,128,128]{3,2,1,0:T(8,128)(2,1)} copy(bf16[3,64,128,128]{3,2,0,1:T(8,128)(2,1)S(1)} %get-tuple-element.6) | data formatting | bytes 12582912 | tf_op jit(solution)/shard_map/jit(_take)/select_n | solution.py:65
  206.0 4.0 %copy.32 = bf16[3,64,128,128]{3,2,1,0:T(8,128)(2,1)} copy(bf16[3,64,128,128]{3,2,0,1:T(8,128)(2,1)S(1)} %get-tuple-element.7) | data formatting | bytes 12582912 | tf_op jit(solution)/shard_map/jit(_take)/select_n | solution.py:68
  210.0 10.3 %bitcast_reduce_fusion = (f32[3,4,128]{2,1,0:T(4,128)S(1)}, bf16[3,4,2048,128]{3,2,1,0:T(8,128)(2,1)}) fusion(pred[4,2048]{1,0:T(4,128)(4,1)S(1)} %bitcast.72, bf16[3,4,2048,128]{3,2,1,0:T(8,128)(2,1)} %bitcast.54, bf16[3,4,128,128]{3,2,1,0:T(8,128)(2,1)S(1)} %bitcast.66), kind=kOutput, calls=%fused_computation.3 | convolution fusion | flops 1632634880 | bytes 12990464 | tf_op jit(solution)/shard_map/sub | solution.py:28
  220.3 6.6 %fusion.10 = bf16[3,4,128,128]{3,2,1,0:T(8,128)(2,1)S(1)} fusion(bf16[3,4,2048,128]{3,2,1,0:T(8,128)(2,1)} %bitcast.55, f32[3,4,128]{2,1,0:T(4,128)S(1)} %get-tuple-element.8, bf16[3,4,2048,128]{3,2,1,0:T(8,128)(2,1)} %get-tuple-element.9), kind=kOutput, calls=%fused_computation.17 | convolution fusion | flops 805699584 | bytes 12982272 | tf_op jit(solution)/shard_map/hbqk,hbkd->hbqd/dot_general | solution.py:30
  227.0 0.2 copy.34
  227.2 0.0 copy-done
  227.2 3.5 %convolution_convert_fusion = bf16[512,3072]{1,0:T(8,128)(2,1)} fusion(bf16[512,384]{0,1:T(8,128)(2,1)S(1)} %bitcast.71, bf16[384,3072]{1,0:T(8,128)(2,1)S(1)} %copy-done), kind=kOutput, calls=%fused_computation.15 | convolution fusion | flops 1209532416 | bytes 5898240 | tf_op jit(solution)/shard_map/dot_general | solution.py:79
  230.6 0.0 reduce-scatter.2.cloned.1.call-update
  230.7 84.3 %reduce-scatter.2.cloned.1.call-done = bf16[64,3072]{1,0:T(8,128)(2,1)} async-done(((bf16[512,3072]{1,0:T(8,128)(2,1)}), bf16[64,3072]{1,0:T(8,128)(2,1)}) %reduce-scatter.2.cloned.1.call-update) | async-done | bytes 393232 | tf_op jit(solution)/shard_map/reduce_scatter | solution.py:78
  (6 shorter events, 0.0 us)
Async XLA Ops:
  6.5 220.6 %copy-start = (bf16[384,3072]{1,0:T(8,128)(2,1)S(1)}, bf16[384,3072]{1,0:T(8,128)(2,1)}, u32[]{:S(2)}) copy-start(bf16[384,3072]{1,0:T(8,128)(2,1)} %param.10) | copy-start | bytes 7077892
  6.5 38.8 %copy-start.1 = (s32[4,16]{1,0:T(4,128)S(1)}, s32[4,16]{1,0:T(4,128)}, u32[]{:S(2)}) copy-start(s32[4,16]{1,0:T(4,128)} %param.11) | copy-start | bytes 772
  6.5 100.6 %all-gather.3.cloned.1.call-start = ((), (), s32[]{:S(2)}) async-start(), calls=%async_computation.4 | async-start | bytes 12976128 | tf_op jit(solution)/shard_map/all_gather | solution.py:58
  24.5 163.4 %all-gather.5.cloned.1.call-start = ((), (), s32[]{:S(2)}) async-start(), calls=%async_computation.5 | async-start | bytes 12976128 | tf_op jit(solution)/shard_map/all_gather | solution.py:59
  40.5 16.8 %all-to-all-start.1 = ((bf16[64,8,384]{2,0,1:T(8,128)(2,1)}), bf16[64,8,384]{2,0,1:T(8,128)(2,1)S(1)}, u32[]{:S(2)}, u32[]{:S(2)}) async-start(bf16[64,8,384]{2,0,1:T(8,128)(2,1)} %bitcast.51), calls=%async_computation.1 | async-start | bytes 786432 | tf_op jit(solution)/shard_map/all_to_all | solution.py:41
  45.3 269.6 %reduce-scatter.2.cloned.1.call-start = ((), (), s32[]{:S(2)}) async-start(), calls=%async_computation.6 | async-start | bytes 3538944 | tf_op jit(solution)/shard_map/reduce_scatter | solution.py:78
Sparse Core Ops, SparseCore 0:
  24.6 82.4 all-gather.2
  109.0 78.8 all-gather.4
  230.8 84.1 reduce-scatter.1
where the time goes:
time: 322 us; the launch traced here: 321 us
  waiting for transfers between devices  218 us (68%)
  local copies, waits for them, and re-layouts  31.6 us (10%)
  blocking collectives  27.9 us (9%)
  matrix products  20.4 us (6%)
  between operations  13.2 us (4%)
  other arithmetic  5.58 us (2%)
  starting transfers between devices  4.92 us (2%)
    reduce_scatter x1, waiting for transfers between devices, on_device(): lax.psum_scatter(jnp.dot(attended, out_weight, preferred_element_type=jnp...  84.3 us
    all_gather x1, waiting for transfers between devices, on_device(): lax.all_gather(value_heads, 'blk', axis=1, tiled=True)  72.1 us
    all_gather x1, waiting for transfers between devices, on_device(): lax.all_gather(key_heads, 'blk', axis=1, tiled=True)  49.7 us
    all_to_all x1, blocking collectives, on_device(): lax.all_to_all(key_tokens, 'head', split_axis=1, concat_axis=0, tiled=True)  15.8 us
    all_to_all x1, blocking collectives, on_device(): lax.all_to_all(value_tokens, 'head', split_axis=1, concat_axis=0, tiled=T...  12 us
    all_to_all x1, waiting for transfers between devices, on_device(): lax.all_to_all(query_tokens, 'head', split_axis=1, concat_axis=0, tiled=T...  11.7 us
    sub x1, matrix products, sparse_attend(): weights = jnp.where(mask_full, jnp.exp(scores - peak_value), 0.0)  10.3 us
    gather x1, local copies, waits for them, and re-layouts, on_device(): jnp.take(source_keys, flat_index, axis=1)  8.63 us
  transfers between devices with their start and end apart: 4, of which 4 were waited for; matrix products, arithmetic and copies ran while one was open for 4% of the time, Pallas kernels for 0%

commit v1 on v0

v1 whole, which is shorter than its diff:
```python
import functools
import math

import jax
import jax.numpy as jnp
from jax import lax
from jax.experimental import pallas as pl
from jax.experimental.pallas import tpu as pltpu
from jax.sharding import PartitionSpec as P

HD = 128
BLK = 128
HEADS_DEV = 3
MESH = pl.DeviceIdType.MESH
ABSENT = -(2.0**100)
SCALE = 1.0 / math.sqrt(HD)

OWN, M1, P1, M2, P2, MIR, TMP = range(7)
UP = {1: M1, 2: M2, 3: TMP, 4: MIR}
DOWN = {1: P1, 2: P2, 3: TMP, 4: MIR}
ORDER = [
    ("A", 0, 1), ("B", 0, 1), ("A", 0, 2), ("B", 0, 2), ("A", 0, 3), ("A", 1, 1),
    ("A", 0, 4), ("B", 1, 1), ("A", 1, 2), ("B", 1, 2), ("A", 1, 3), ("A", 2, 1),
    ("A", 1, 4), ("B", 2, 1), ("A", 2, 2), ("B", 2, 2), ("A", 2, 3), ("A", 2, 4),
]
WORK = {
    8: [("unit", 0, 3)], 9: [("unit", 0, 2)], 10: [("unit", 0, 1)], 11: [("unit", 0, 0)],
    13: [("merge", 0)],
    14: [("unit", 1, 3)], 15: [("unit", 1, 2)], 16: [("unit", 1, 1)],
    17: [("unit", 1, 0), ("merge", 1), ("unit", 2, 3), ("unit", 2, 2), ("unit", 2, 1), ("unit", 2, 0), ("merge", 2)],
}


def kernel(q_hbm, k_hbm, v_hbm, kvb_ref, out_ref, *scratch):
    nh = HEADS_DEV
    kb, vb, qb_, os_, or_ = (scratch[i * nh : (i + 1) * nh] for i in range(5))
    kvb_all, kvb_smem, a_send, a_recv, zs, zr, qs, qr, osem, orsem, misc = scratch[5 * nh :]
    b = lax.axis_index("blk")
    g = lax.axis_index("head")
    z, r = lax.div(b, 4), lax.rem(b, 4)
    xl, c = lax.div(r, 2), lax.rem(r, 2)
    ghalf, glow = lax.div(g, 2), lax.rem(g, 2)
    plane = [(xl, c), (xl, 1 - c), (1 - xl, c), (1 - xl, 1 - c)]
    plane_r = [x * 2 + cc for x, cc in plane]
    plane_dev = [(z * 4 + rr, g) for rr in plane_r]
    zdev = {"U": (lax.rem(z + 1, 8) * 4 + r, g), "D": (lax.rem(z + 7, 8) * 4 + r, g)}

    def head_dev(d):
        return lax.rem(g + d, 8)

    barrier = pltpu.get_barrier_semaphore()
    for dev in plane_dev[1:] + list(zdev.values()) + [(b, head_dev(d)) for d in range(1, 8)]:
        pl.semaphore_signal(barrier, inc=1, device_id=dev, device_id_type=MESH)
    pl.semaphore_wait(barrier, 12)

    def wait_bytes(ref, sem):
        pltpu.make_async_copy(ref, ref, sem).wait()

    done = set()

    src = {"K": k_hbm, "V": v_hbm, "Q": q_hbm}

    def a2a_dst(x, h):
        if x == "Q":
            return qb_[h], r * 4
        return (kb if x == "K" else vb)[h], OWN * 4

    a2a_idx = {}
    for h in range(nh):
        for x in "KVQ":
            a2a_idx[x, h] = len(a2a_idx)

    def a2a_start(x, h):
        i = a2a_idx[x, h]
        buf, base = a2a_dst(x, h)
        dst = buf.at[base + ghalf, pl.ds(pl.multiple_of(glow * 64, 64), 64), :]

        def cols(dest):
            return src[x].at[:, pl.ds(pl.multiple_of(dest * (nh * HD) + h * HD, HD), HD)]

        pltpu.make_async_copy(cols(g), dst, a_recv.at[i]).start()

        def one(d, carry):
            dest = head_dev(d)
            pltpu.make_async_remote_copy(
                src_ref=cols(dest), dst_ref=dst, send_sem=a_send.at[i], recv_sem=a_recv.at[i],
                device_id=(b, dest), device_id_type=MESH,
            ).start()
            return carry

        lax.fori_loop(1, 8, one, 0)

    def a2a_wait(x, h):
        if ("a2a", x, h) in done:
            return
        done.add(("a2a", x, h))
        buf, base = a2a_dst(x, h)
        wait_bytes(buf.at[pl.ds(base, 4)], a_recv.at[a2a_idx[x, h]])

    kv_copies = []
    for i in range(1, 4):
        kv_copies.append(
            pltpu.make_async_remote_copy(
                src_ref=kvb_ref, dst_ref=kvb_all.at[r], send_sem=misc.at[2 * i], recv_sem=misc.at[2 * i + 1],
                device_id=plane_dev[i], device_id_type=MESH,
            )
        )
    kv_own = pltpu.make_async_copy(kvb_ref, kvb_all.at[r], misc.at[0])

    for x, h in list(a2a_idx)[:2]:
        a2a_start(x, h)
    kv_own.start()
    for cp in kv_copies:
        cp.start()
    for x, h in list(a2a_idx)[2:]:
        a2a_start(x, h)

    def tensor(direction, kind):
        return kb if (direction == "U") == (kind == "A") else vb

    zname = {}

    def zcopy(direction, n):
        kind, h, hop = ORDER[n]
        slots = UP if direction == "U" else DOWN
        buf = tensor(direction, kind)[h]
        s_src = OWN if hop == 1 else slots[hop - 1]
        s_dst = slots[hop]
        k = n + (len(ORDER) if direction == "D" else 0)
        return pltpu.make_async_remote_copy(
            src_ref=buf.at[pl.ds(s_src * 4, 4)], dst_ref=buf.at[pl.ds(s_dst * 4, 4)],
            send_sem=zs.at[k], recv_sem=zr.at[k], device_id=zdev[direction], device_id_type=MESH,
        )

    def z_wait(direction, n):
        if ("z", direction, n) in done:
            return
        done.add(("z", direction, n))
        zcopy(direction, n).wait_recv()

    def z_step(direction, n):
        kind, h, hop = ORDER[n]
        if hop == 1:
            is_k = (direction == "U") == (kind == "A")
            a2a_wait("K" if is_k else "V", h)
        else:
            z_wait(direction, ORDER.index((kind, h, hop - 1)))
        zcopy(direction, n).start()

    def q_copy(h, i):
        ref = qb_[h].at[pl.ds(r * 4, 4)]
        return pltpu.make_async_remote_copy(
            src_ref=ref, dst_ref=ref, send_sem=qs.at[h * 3 + i - 1], recv_sem=qr.at[h * 3 + i - 1],
            device_id=plane_dev[i], device_id_type=MESH,
        )

    def q_send(h):
        a2a_wait("Q", h)
        for i in (3, 2, 1):
            q_copy(h, i).start()

    def q_wait(h):
        if ("q", h) in done:
            return
        done.add(("q", h))
        for i in (1, 2, 3):
            ref = qb_[h].at[pl.ds(plane_r[i] * 4, 4)]
            wait_bytes(ref, qr.at[h * 3 + i - 1])

    def kvb_wait():
        if "kvb" in done:
            return
        done.add("kvb")
        kv_own.wait()
        for i in range(1, 4):
            kv_copies[i - 1].wait()
        cp = pltpu.make_async_copy(kvb_all, kvb_smem, misc.at[1])
        cp.start()
        cp.wait()

    lane = lax.broadcasted_iota(jnp.int32, (BLK, BLK), 1)

    def o_copy(h, i):
        return pltpu.make_async_remote_copy(
            src_ref=os_[h].at[i], dst_ref=or_[h].at[i], send_sem=osem.at[h * 4 + i], recv_sem=orsem.at[h * 4 + i],
            device_id=plane_dev[i], device_id_type=MESH,
        )

    def unit(h, i):
        kvb_wait()
        q_wait(h)
        for x in "KV":
            a2a_wait(x, h)
        for n, (_, hh, _) in enumerate(ORDER):
            if hh == h:
                z_wait("U", n)
                z_wait("D", n)
        rq = plane_r[i]
        dl = r - rq
        gt = lax.div(dl + 3, 4)
        lt = lax.div(3 - dl, 4)
        eq = 1 - gt - lt
        picks = [
            (OWN, gt * (2 * dl) + lt * (1 - 2 * dl)),
            (M1, 9 - 2 * dl),
            (P1, 2 * dl + 8),
            (M2 * gt + P2 * lt + MIR * eq, gt * (17 - 2 * dl) + lt * (2 * dl + 16) + eq),
        ]

        def block(j, stats):
            q = qb_[h][rq * 4 + j]
            scores, vals = [], []
            for slot, col in picks:
                e = kvb_smem[rq, j, col]
                idx = slot * 4 + jnp.bitwise_and(e, 3)
                bias = jnp.where(e >= 0, 0.0, ABSENT).astype(jnp.float32)
                s = lax.dot_general(q, kb[h][idx], (((1,), (1,)), ((), ())), preferred_element_type=jnp.float32)
                scores.append(s * SCALE + bias)
                vals.append(vb[h][idx])
            top = functools.reduce(jnp.maximum, scores)
            m = jnp.max(top, axis=1, keepdims=True).astype(jnp.bfloat16).astype(jnp.float32)
            ps = [jnp.exp(s - m) for s in scores]
            l = jnp.sum(functools.reduce(jnp.add, ps), axis=1, keepdims=True)
            o = functools.reduce(
                jnp.add,
                [
                    jnp.dot(p.astype(jnp.bfloat16), v, preferred_element_type=jnp.float32)
                    for p, v in zip(ps, vals)
                ],
            )
            os_[h][i, j] = o.astype(jnp.bfloat16)
            l_hi = l.astype(jnp.bfloat16).astype(jnp.float32)
            stats = jnp.where(lane == j, m, stats)
            stats = jnp.where(lane == j + 4, l_hi, stats)
            return jnp.where(lane == j + 8, l - l_hi, stats)

        stats = lax.fori_loop(0, 4, block, jnp.zeros((BLK, BLK), jnp.float32))
        os_[h][i, 4] = stats.astype(jnp.bfloat16)
        if i:
            o_copy(h, i).start()

    def merge(h):
        for i in (1, 2, 3):
            o_copy(h, i).wait_recv()
        bufs = [os_[h].at[0]] + [or_[h].at[i] for i in (1, 2, 3)]
        stats = [bf[4].astype(jnp.float32) for bf in bufs]
        for j in range(4):
            ms = [s[:, j : j + 1] for s in stats]
            ls = [s[:, j + 4 : j + 5] + s[:, j + 8 : j + 9] for s in stats]
            top = functools.reduce(jnp.maximum, ms)
            ws = [jnp.exp(m - top) for m in ms]
            inv = 1.0 / functools.reduce(jnp.add, [w * l for w, l in zip(ws, ls)])
            o = functools.reduce(
                jnp.add, [(w * inv) * bf[j].astype(jnp.float32) for w, bf in zip(ws, bufs)]
            )
            out_ref[j * BLK : (j + 1) * BLK, h * HD : (h + 1) * HD] = o.astype(jnp.bfloat16)

    for n in range(len(ORDER)):
        z_step("U", n)
        z_step("D", n)
        if n in (3, 7, 11):
            q_send((n - 3) // 4)
        for job in WORK.get(n, ()):
            if job[0] == "unit":
                unit(job[1], job[2])
            else:
                merge(job[1])

    for n in range(len(ORDER)):
        for direction in "UD":
            zcopy(direction, n).wait_send()
    for h in range(nh):
        for i in (1, 2, 3):
            q_copy(h, i).wait_send()
            o_copy(h, i).wait_send()
    for (x, h), i in a2a_idx.items():
        wait_bytes(src[x].at[:, pl.ds(0, 7 * HD)], a_send.at[i])


def on_device(query_tokens, key_tokens, value_tokens, out_weight, kv_blocks):
    nh = HEADS_DEV
    rows = query_tokens.shape[0] * 8
    lists = jnp.pad(kv_blocks, ((0, 4), (0, 128 - kv_blocks.shape[1])), constant_values=-1)
    any_spec = pl.BlockSpec(memory_space=pl.ANY)
    vm = pl.BlockSpec(memory_space=pltpu.VMEM)
    bf = jnp.bfloat16
    dma = pltpu.SemaphoreType.DMA
    attended = pl.pallas_call(
        kernel,
        out_shape=jax.ShapeDtypeStruct((rows, nh * HD), bf),
        in_specs=[any_spec, any_spec, any_spec, vm],
        out_specs=vm,
        scratch_shapes=[pltpu.VMEM((28, BLK, HD), bf)] * (2 * nh)
        + [pltpu.VMEM((16, BLK, HD), bf)] * nh
        + [pltpu.VMEM((4, 5, BLK, HD), bf)] * (2 * nh)
        + [
            pltpu.VMEM((4, 8, 128), jnp.int32),
            pltpu.SMEM((4, 8, 128), jnp.int32),
            dma((9,)), dma((9,)),
            dma((36,)), dma((36,)),
            dma((9,)), dma((9,)),
            dma((12,)), dma((12,)),
            dma((8,)),
        ],
        compiler_params=pltpu.CompilerParams(
            collective_id=0, has_side_effects=True, vmem_limit_bytes=48 << 20
        ),
        name="attend",
    )(query_tokens, key_tokens, value_tokens, lists)
    return lax.psum_scatter(
        jnp.dot(attended, out_weight, preferred_element_type=jnp.float32).astype(jnp.bfloat16),
        "head",
        scatter_dimension=0,
        tiled=True,
    )


def solution(mesh):
    placed = (
        P(("blk", "head"), None),
        P(("blk", "head"), None),
        P(("blk", "head"), None),
        P("head", None),
        P("blk", None),
    )
    return jax.shard_map(
        on_device, mesh=mesh, in_specs=placed, out_specs=P(("blk", "head"), None), check_vma=False
    )
```

time: 322 us -> 182 us (0.57)
  waiting for transfers between devices: 218 us -> 82.8 us
  Pallas kernels: 0 us -> 78.2 us
  blocking collectives: 27.9 us -> 0 us
  local copies, waits for them, and re-layouts: 31.6 us -> 3.83 us
  matrix products: 20.4 us -> 3.47 us
  other arithmetic: 5.58 us -> 0 us
  starting transfers between devices: 4.92 us -> 0.01 us
    all_gather x2 -> x0, waiting for transfers between devices: 122 us -> none  [the longest x1 72.1 us: on_device(): lax.all_gather(value_heads, 'blk', axis=1, tiled=True)]
    pallas_call x0 -> x1, Pallas kernels: none -> 78.2 us  [on_device(): pl.pallas_call(kernel, out_shape=jax.ShapeDtypeStruct((rows, nh * HD), bf...]
    all_to_all x2 -> x0, blocking collectives: 27.9 us -> none  [the longest x1 15.8 us: on_device(): lax.all_to_all(key_tokens, 'head', split_axis=1, concat_axis=0, tiled=True)]
    gather x2 -> x0, local copies, waits for them, and re-layouts: 17.2 us -> none  [the longest x1 8.63 us: on_device(): jnp.take(source_keys, flat_index, axis=1)]
    all_to_all x1 -> x0, waiting for transfers between devices: 11.7 us -> none  [on_device(): lax.all_to_all(query_tokens, 'head', split_axis=1, concat_axis=0, tiled=T...]
    sub x1 -> x0, matrix products: 10.3 us -> none  [sparse_attend(): weights = jnp.where(mask_full, jnp.exp(scores - peak_value), 0.0)]
    select_n x2 -> x0, local copies, waits for them, and re-layouts: 8.03 us -> none  [the longest x1 4.03 us: on_device(): jnp.take(source_values, flat_index, axis=1)]
    dot_general x1 -> x0, matrix products: 6.63 us -> none  [sparse_attend(): jnp.einsum('hbqk,hbkd->hbqd', weights.astype(jnp.bfloat16), value_sets, p...]
  transfers between devices with their start and end apart: 4 -> 1, of which waited for: 4 -> 1; matrix products, arithmetic and copies ran while one was open for 4% -> 0% of each run, Pallas kernels for 0% -> 0%
where the time goes in v1:
time: 182 us
  waiting for transfers between devices  82.8 us (45%)
  Pallas kernels  78.2 us (43%)
  between operations  13.4 us (7%)
  local copies, waits for them, and re-layouts  3.83 us (2%)
  matrix products  3.47 us (2%)
    reduce_scatter x1, waiting for transfers between devices, on_device(): lax.psum_scatter(jnp.dot(attended, out_weight, preferred_element_type=jnp...  82.8 us
    pallas_call x1, Pallas kernels, on_device(): pl.pallas_call(kernel, out_shape=jax.ShapeDtypeStruct((rows, nh * HD), bf...  78.2 us
  transfers between devices with their start and end apart: 1, of which 1 were waited for; matrix products, arithmetic and copies ran while one was open for 0% of the time, Pallas kernels for 0%

profile of v1, /device:TPU:8, one launch (start us, length us, event | category | flops | bytes accessed | tf_op | source)
XLA Modules:
  0.0 181.7 jit_solution(5379389488609014278)
XLA Ops:
  6.5 0.0 copy-start
  6.5 0.0 reduce-scatter.2.cloned.1.call-start
  6.5 0.8 pad.4.kvb_ref
  7.4 0.0 copy-start.1
  7.4 1.0 copy-done.1
  8.4 0.0 copy-start.2
  8.4 1.0 copy-done.2
  9.4 0.0 copy-start.3
  9.4 1.0 copy-done.3
  10.4 78.2 %attend.1 = bf16[512,384]{1,0:T(8,128)(2,1)S(1)} custom-call(bf16[64,3072]{1,0:T(8,128)(2,1)S(1)} %copy-done.1, bf16[64,3072]{1,0:T(8,128)(2,1)S(1)} %copy-done.2, bf16[64,3072]{1,0:T(8,128)(2,1)S(1)} %copy-done.3, s32[8,128]{1,0:T(8,128)S(1)} %pad.4.kvb_ref), custom_call_target="tpu_custom_call" | custom-call | tf_op jit(solution)/shard_map/attend/pallas_call | solution.py:288
  88.6 0.0 copy-done
  88.6 3.5 %convolution_convert_fusion = bf16[512,3072]{1,0:T(8,128)(2,1)} fusion(bf16[512,384]{1,0:T(8,128)(2,1)S(1)} %attend.1, bf16[384,3072]{1,0:T(8,128)(2,1)S(1)} %copy-done), kind=kOutput, calls=%fused_computation | convolution fusion | flops 1209532416 | bytes 5898240 | tf_op jit(solution)/shard_map/dot_general | solution.py:311
  92.1 0.0 reduce-scatter.2.cloned.1.call-update
  92.1 82.8 %reduce-scatter.2.cloned.1.call-done = bf16[64,3072]{1,0:T(8,128)(2,1)} async-done(((bf16[512,3072]{1,0:T(8,128)(2,1)}), bf16[64,3072]{1,0:T(8,128)(2,1)}) %reduce-scatter.2.cloned.1.call-update) | async-done | bytes 393232 | tf_op jit(solution)/shard_map/reduce_scatter | solution.py:310
Async XLA Ops:
  6.5 82.1 %copy-start = (bf16[384,3072]{1,0:T(8,128)(2,1)S(1)}, bf16[384,3072]{1,0:T(8,128)(2,1)}, u32[]{:S(2)}) copy-start(bf16[384,3072]{1,0:T(8,128)(2,1)} %param.8) | copy-start | bytes 7077892
  6.5 168.3 %reduce-scatter.2.cloned.1.call-start = ((), (), s32[]{:S(2)}) async-start(), calls=%async_computation.1 | async-start | bytes 3538944 | tf_op jit(solution)/shard_map/reduce_scatter | solution.py:310
  7.4 1.0 copy-start.1
  8.4 1.0 copy-start.2
  9.4 1.0 copy-start.3
Sparse Core Ops, SparseCore 0:
  92.2 82.5 reduce-scatter.1

commit v2 on v1

--- a/solution.py
+++ b/solution.py
@@ -19,22 +19,33 @@
 UP = {1: M1, 2: M2, 3: TMP, 4: MIR}
 DOWN = {1: P1, 2: P2, 3: TMP, 4: MIR}
 ORDER = [
-    ("A", 0, 1), ("B", 0, 1), ("A", 0, 2), ("B", 0, 2), ("A", 0, 3), ("A", 1, 1),
-    ("A", 0, 4), ("B", 1, 1), ("A", 1, 2), ("B", 1, 2), ("A", 1, 3), ("A", 2, 1),
+    ("A", 0, 1), ("B", 0, 1), ("A", 0, 2), ("B", 0, 2), ("A", 1, 1), ("A", 0, 3),
+    ("B", 1, 1), ("A", 1, 2), ("A", 0, 4), ("B", 1, 2), ("A", 1, 3), ("A", 2, 1),
     ("A", 1, 4), ("B", 2, 1), ("A", 2, 2), ("B", 2, 2), ("A", 2, 3), ("A", 2, 4),
 ]
 WORK = {
-    8: [("unit", 0, 3)], 9: [("unit", 0, 2)], 10: [("unit", 0, 1)], 11: [("unit", 0, 0)],
-    13: [("merge", 0)],
-    14: [("unit", 1, 3)], 15: [("unit", 1, 2)], 16: [("unit", 1, 1)],
-    17: [("unit", 1, 0), ("merge", 1), ("unit", 2, 3), ("unit", 2, 2), ("unit", 2, 1), ("unit", 2, 0), ("merge", 2)],
+    0: ["a2a Q0", "a2a K1", "a2a V1"],
+    1: ["a2a K2", "a2a V2", "a2a Q1", "a2a Q2", "wown", "w1 2", "xo0"],
+    2: ["qsend 0"],
+    3: ["w1 0", "qfwd 0"],
+    6: ["unit 0 3", "unit 0 2", "qsend 1"],
+    7: ["unit 0 1", "qfwd 1"],
+    8: ["w1r 2", "w1 1"],
+    9: ["xor 0", "qsend 2"],
+    10: ["qfwd 2"],
+    11: ["unit 0 0", "merge 0", "w1r 0", "unit 1 3", "unit 1 2"],
+    12: ["unit 1 1", "w2r 2"],
+    14: ["w1r 1", "unit 1 0", "merge 1"],
+    15: ["w2r 0", "xor 1", "xor 2"],
+    16: ["unit 2 3", "unit 2 2", "xor 3"],
+    17: ["unit 2 1", "w2r 1", "proj 0", "proj 1", "unit 2 0", "merge 2", "final"],
 }
 
 
-def kernel(q_hbm, k_hbm, v_hbm, kvb_ref, out_ref, *scratch):
+def kernel(q_hbm, k_hbm, v_hbm, w_hbm, kvb_ref, out_ref, *scratch):
     nh = HEADS_DEV
-    kb, vb, qb_, os_, or_ = (scratch[i * nh : (i + 1) * nh] for i in range(5))
-    kvb_all, kvb_smem, a_send, a_recv, zs, zr, qs, qr, osem, orsem, misc = scratch[5 * nh :]
+    kb, vb, qb_, os_, or_, wb, att, ab, km, vm = (scratch[i * nh : (i + 1) * nh] for i in range(10))
+    (kvb_all, kvb_smem, pacc, pb, prec, a_send, a_recv, zs, zr, qs, qr, osem, orsem, misc, ws, wr, ts, tr) = scratch[10 * nh :]
     b = lax.axis_index("blk")
     g = lax.axis_index("head")
     z, r = lax.div(b, 4), lax.rem(b, 4)
@@ -43,15 +54,18 @@
     plane = [(xl, c), (xl, 1 - c), (1 - xl, c), (1 - xl, 1 - c)]
     plane_r = [x * 2 + cc for x, cc in plane]
     plane_dev = [(z * 4 + rr, g) for rr in plane_r]
+    xh, y = lax.div(g, 4), lax.rem(g, 4)
+    xo_dev = (z * 4 + (1 - xl) * 2 + c, (1 - xh) * 4 + y)
+    xh_dev = (b, (1 - xh) * 4 + y)
     zdev = {"U": (lax.rem(z + 1, 8) * 4 + r, g), "D": (lax.rem(z + 7, 8) * 4 + r, g)}
 
     def head_dev(d):
         return lax.rem(g + d, 8)
 
     barrier = pltpu.get_barrier_semaphore()
-    for dev in plane_dev[1:] + list(zdev.values()) + [(b, head_dev(d)) for d in range(1, 8)]:
+    for dev in plane_dev[1:] + list(zdev.values()) + [(b, head_dev(d)) for d in range(1, 8)] + [xo_dev]:
         pl.semaphore_signal(barrier, inc=1, device_id=dev, device_id_type=MESH)
-    pl.semaphore_wait(barrier, 12)
+    pl.semaphore_wait(barrier, 13)
 
     def wait_bytes(ref, sem):
         pltpu.make_async_copy(ref, ref, sem).wait()
@@ -112,23 +126,24 @@
     kv_own.start()
     for cp in kv_copies:
         cp.start()
-    for x, h in list(a2a_idx)[2:]:
-        a2a_start(x, h)
 
     def tensor(direction, kind):
-        return kb if (direction == "U") == (kind == "A") else vb
+        return (kb, km) if (direction == "U") == (kind == "A") else (vb, vm)
+
+    def slot_ref(bufs, h, slot):
+        return bufs[0][h].at[pl.ds(slot * 4, 4)] if slot < MIR else bufs[1][h].at[pl.ds((slot - MIR) * 4, 4)]
 
     zname = {}
 
     def zcopy(direction, n):
         kind, h, hop = ORDER[n]
         slots = UP if direction == "U" else DOWN
-        buf = tensor(direction, kind)[h]
+        bufs = tensor(direction, kind)
         s_src = OWN if hop == 1 else slots[hop - 1]
         s_dst = slots[hop]
         k = n + (len(ORDER) if direction == "D" else 0)
         return pltpu.make_async_remote_copy(
-            src_ref=buf.at[pl.ds(s_src * 4, 4)], dst_ref=buf.at[pl.ds(s_dst * 4, 4)],
+            src_ref=slot_ref(bufs, h, s_src), dst_ref=slot_ref(bufs, h, s_dst),
             send_sem=zs.at[k], recv_sem=zr.at[k], device_id=zdev[direction], device_id_type=MESH,
         )
 
@@ -148,24 +163,26 @@
         zcopy(direction, n).start()
 
     def q_copy(h, i):
-        ref = qb_[h].at[pl.ds(r * 4, 4)]
+        ref = qb_[h].at[pl.ds(plane_r[2 if i == 3 else 0] * 4, 4)]
         return pltpu.make_async_remote_copy(
             src_ref=ref, dst_ref=ref, send_sem=qs.at[h * 3 + i - 1], recv_sem=qr.at[h * 3 + i - 1],
-            device_id=plane_dev[i], device_id_type=MESH,
+            device_id=plane_dev[2 if i == 2 else 1], device_id_type=MESH,
         )
 
     def q_send(h):
         a2a_wait("Q", h)
-        for i in (3, 2, 1):
+        for i in (2, 1):
             q_copy(h, i).start()
 
-    def q_wait(h):
-        if ("q", h) in done:
-            return
-        done.add(("q", h))
-        for i in (1, 2, 3):
-            ref = qb_[h].at[pl.ds(plane_r[i] * 4, 4)]
-            wait_bytes(ref, qr.at[h * 3 + i - 1])
+    def q_fwd(h):
+        q_wait(h, (2,))
+        q_copy(h, 3).start()
+
+    def q_wait(h, which=(1, 2, 3)):
+        for i in which:
+            if ("q", h, i) not in done:
+                done.add(("q", h, i))
+                wait_bytes(qb_[h].at[pl.ds(plane_r[i] * 4, 4)], qr.at[h * 3 + i - 1])
 
     def kvb_wait():
         if "kvb" in done:
@@ -191,8 +208,8 @@
         q_wait(h)
         for x in "KV":
             a2a_wait(x, h)
-        for n, (_, hh, _) in enumerate(ORDER):
-            if hh == h:
+        for n, (_, hh, hop) in enumerate(ORDER):
+            if hh == h and hop in ((1, 2, 4) if i == 0 else (1, 2)):
                 z_wait("U", n)
                 z_wait("D", n)
         rq = plane_r[i]
@@ -204,19 +221,20 @@
             (OWN, gt * (2 * dl) + lt * (1 - 2 * dl)),
             (M1, 9 - 2 * dl),
             (P1, 2 * dl + 8),
-            (M2 * gt + P2 * lt + MIR * eq, gt * (17 - 2 * dl) + lt * (2 * dl + 16) + eq),
+            (0 if i == 0 else M2 * gt + P2 * lt, gt * (17 - 2 * dl) + lt * (2 * dl + 16) + eq),
         ]
 
         def block(j, stats):
             q = qb_[h][rq * 4 + j]
             scores, vals = [], []
-            for slot, col in picks:
+            for n, (slot, col) in enumerate(picks):
+                keys, values = (km[h], vm[h]) if n == 3 and i == 0 else (kb[h], vb[h])
                 e = kvb_smem[rq, j, col]
                 idx = slot * 4 + jnp.bitwise_and(e, 3)
                 bias = jnp.where(e >= 0, 0.0, ABSENT).astype(jnp.float32)
-                s = lax.dot_general(q, kb[h][idx], (((1,), (1,)), ((), ())), preferred_element_type=jnp.float32)
+                s = lax.dot_general(q, keys[idx], (((1,), (1,)), ((), ())), preferred_element_type=jnp.float32)
                 scores.append(s * SCALE + bias)
-                vals.append(vb[h][idx])
+                vals.append(values[idx])
             top = functools.reduce(jnp.maximum, scores)
             m = jnp.max(top, axis=1, keepdims=True).astype(jnp.bfloat16).astype(jnp.float32)
             ps = [jnp.exp(s - m) for s in scores]
@@ -253,18 +271,183 @@
             o = functools.reduce(
                 jnp.add, [(w * inv) * bf[j].astype(jnp.float32) for w, bf in zip(ws, bufs)]
             )
-            out_ref[j * BLK : (j + 1) * BLK, h * HD : (h + 1) * HD] = o.astype(jnp.bfloat16)
+            att[h][j * BLK : (j + 1) * BLK, :] = o.astype(jnp.bfloat16)
+        att_copies(h)
+
+    def att_copies(h):
+        def rows(gg):
+            return att[h].at[pl.ds(pl.multiple_of(gg * 64, 64), 64), :]
+
+        if h < 2:
+            col = pl.ds(pl.multiple_of(y * HD, HD), HD)
+            for p in range(2):
+                dst = ab[h].at[p, :, col]
+                pltpu.make_async_copy(rows(p * 4 + y), dst, tr.at[h]).start()
+                for d in (2, 1, 3):
+                    yy = lax.rem(y + d, 4)
+                    pltpu.make_async_remote_copy(
+                        src_ref=rows(p * 4 + yy), dst_ref=dst, send_sem=ts.at[h], recv_sem=tr.at[h],
+                        device_id=(b, xh * 4 + yy), device_id_type=MESH,
+                    ).start()
+        else:
+            dst = ab[h].at[:, pl.ds(pl.multiple_of(g * HD, HD), HD)]
+            pltpu.make_async_copy(rows(g), dst, tr.at[h]).start()
+            for d in range(1, 8):
+                gg = head_dev(d)
+                pltpu.make_async_remote_copy(
+                    src_ref=rows(gg), dst_ref=dst, send_sem=ts.at[h], recv_sem=tr.at[h],
+                    device_id=(b, gg), device_id_type=MESH,
+                ).start()
+
+    half = w_hbm.shape[1] // 2
+    wcol = pl.ds(pl.multiple_of(c * half, 128), half)
+    ocol = pl.ds(pl.multiple_of((1 - c) * half, 128), half)
+    ydev = {d: (b, xh * 4 + lax.rem(y + d, 4)) for d in (1, 2, 3)}
+
+    def widx(h, d, other=False):
+        base = 0 if h < 2 else (1 - xh if other else xh) * 4
+        return base + lax.rem(y + d, 4)
+
+    def remote(src_ref, dst_ref, i, dev):
+        return pltpu.make_async_remote_copy(
+            src_ref=src_ref, dst_ref=dst_ref, send_sem=ws.at[i], recv_sem=wr.at[i], device_id=dev, device_id_type=MESH
+        )
+
+    def w_hop1(h, d):
+        return remote(
+            w_hbm.at[h * HD : (h + 1) * HD, wcol], wb[h].at[widx(h, 0), :, wcol], h * 7 + (0 if d == 1 else 1), ydev[d]
+        )
+
+    def w_hop2(h, d):
+        ref = wb[h].at[widx(h, 4 - d), pl.ds(0 if d == 1 else 64, 64), wcol]
+        return remote(ref, ref, h * 7 + (2 if d == 1 else 3), ydev[d])
+
+    def w_sib(h, d):
+        ref = wb[h].at[widx(h, d), :, wcol]
+        return remote(ref, ref, h * 7 + 3 + d, plane_dev[1])
+
+    def x_piece(k):
+        dst = wb[2].at[widx(2, k), :, wcol]
+        return remote(w_hbm.at[2 * HD : 3 * HD, wcol] if k == 0 else dst, dst, 21 + k, xo_dev)
+
+    def x_sib(k):
+        ref = wb[2].at[widx(2, k, True), :, wcol]
+        return remote(ref, ref, 25 + k, plane_dev[1])
+
+    def w_own(h):
+        return pltpu.make_async_copy(w_hbm.at[h * HD : (h + 1) * HD, :], wb[h].at[widx(h, 0)], tr.at[3 + h])
+
+    wsends = []
+
+    def go(cp):
+        cp.start()
+        wsends.append(cp)
+
+    def w_ready(h):
+        w_own(h).wait()
+        for d in (1, 2, 3):
+            wait_bytes(wb[h].at[widx(h, d), :, ocol], wr.at[h * 7 + 3 + d])
+        if h == 2:
+            for k in range(4):
+                wait_bytes(wb[2].at[widx(2, k, True), :, ocol], wr.at[25 + k])
+
+    step = 512
+
+    def columns(t):
+        return pl.ds(pl.multiple_of(t * step, step), step)
+
+    def project(h):
+        w_ready(h)
+        wait_bytes(ab[h], tr.at[h])
+        rows = ab[h][...].reshape(2 * 64, 4 * HD)
+
+        def one(t, carry):
+            col = columns(t)
+            res = jnp.dot(rows, wb[h][:, :, col].reshape(4 * HD, step), preferred_element_type=jnp.float32)
+            if h:
+                res = res + pacc[:, col]
+                pb[:, col] = res.astype(jnp.bfloat16)
+            pacc[:, col] = res
+            return carry
+
+        lax.fori_loop(0, pacc.shape[1] // step, one, 0)
+        if h:
+            p_copy.start()
+
+    p_copy = pltpu.make_async_remote_copy(
+        src_ref=pb.at[pl.ds(pl.multiple_of((1 - xh) * 64, 64), 64), :], dst_ref=prec,
+        send_sem=ts.at[3], recv_sem=tr.at[6], device_id=xh_dev, device_id_type=MESH,
+    )
+
+    def final():
+        w_ready(2)
+        wait_bytes(ab[2], tr.at[2])
+        p_copy.wait_recv()
+        rows = ab[2][...]
+
+        def one(t, carry):
+            col = columns(t)
+            res = jnp.dot(rows, wb[2][:, :, col].reshape(8 * HD, step), preferred_element_type=jnp.float32)
+            mine = pacc[pl.ds(pl.multiple_of(xh * 64, 64), 64), col]
+            out_ref[:, col] = (res + mine + prec[:, col].astype(jnp.float32)).astype(jnp.bfloat16)
+            return carry
+
+        lax.fori_loop(0, pacc.shape[1] // step, one, 0)
+
+    def job(text):
+        name, *rest = text.split(" ")
+        if name == "a2a":
+            a2a_start(rest[0][0], int(rest[0][1]))
+            return
+        v = [int(a) for a in rest]
+        if name == "unit":
+            unit(*v)
+        elif name == "merge":
+            merge(*v)
+        elif name == "proj":
+            project(*v)
+        elif name == "final":
+            final()
+        elif name == "qsend":
+            q_send(*v)
+        elif name == "qfwd":
+            q_fwd(*v)
+        elif name == "wown":
+            for h in range(nh):
+                w_own(h).start()
+        elif name == "w1":
+            go(w_hop1(v[0], 1))
+            go(w_hop1(v[0], 3))
+        elif name == "w1r":
+            h = v[0]
+            w_hop1(h, 1).wait_recv()
+            w_hop1(h, 3).wait_recv()
+            go(w_hop2(h, 1))
+            go(w_hop2(h, 3))
+            go(w_sib(h, 1))
+            go(w_sib(h, 3))
+            if h == 2:
+                go(x_piece(1))
+                go(x_piece(3))
+        elif name == "w2r":
+            h = v[0]
+            w_hop2(h, 1).wait_recv()
+            w_hop2(h, 3).wait_recv()
+            go(w_sib(h, 2))
+            if h == 2:
+                go(x_piece(2))
+        elif name == "xo0":
+            go(x_piece(0))
+        elif name == "xor":
+            k = (0, 1, 3, 2)[v[0]]
+            x_piece(k).wait_recv()
+            go(x_sib(k))
 
     for n in range(len(ORDER)):
         z_step("U", n)
         z_step("D", n)
-        if n in (3, 7, 11):
-            q_send((n - 3) // 4)
-        for job in WORK.get(n, ()):
-            if job[0] == "unit":
-                unit(job[1], job[2])
-            else:
-                merge(job[1])
+        for text in WORK.get(n, ()):
+            job(text)
 
     for n in range(len(ORDER)):
         for direction in "UD":
@@ -275,44 +458,54 @@
             o_copy(h, i).wait_send()
     for (x, h), i in a2a_idx.items():
         wait_bytes(src[x].at[:, pl.ds(0, 7 * HD)], a_send.at[i])
+    for cp in wsends:
+        cp.wait_send()
+    wait_bytes(att[0].at[pl.ds(0, 6 * 64)], ts.at[0])
+    wait_bytes(att[1].at[pl.ds(0, 6 * 64)], ts.at[1])
+    wait_bytes(att[2].at[pl.ds(0, 7 * 64)], ts.at[2])
+    p_copy.wait_send()
 
 
 def on_device(query_tokens, key_tokens, value_tokens, out_weight, kv_blocks):
     nh = HEADS_DEV
-    rows = query_tokens.shape[0] * 8
+    rows, width = query_tokens.shape
     lists = jnp.pad(kv_blocks, ((0, 4), (0, 128 - kv_blocks.shape[1])), constant_values=-1)
     any_spec = pl.BlockSpec(memory_space=pl.ANY)
     vm = pl.BlockSpec(memory_space=pltpu.VMEM)
     bf = jnp.bfloat16
     dma = pltpu.SemaphoreType.DMA
-    attended = pl.pallas_call(
+    return pl.pallas_call(
         kernel,
-        out_shape=jax.ShapeDtypeStruct((rows, nh * HD), bf),
-        in_specs=[any_spec, any_spec, any_spec, vm],
+        out_shape=jax.ShapeDtypeStruct((rows, width), bf),
+        in_specs=[any_spec, any_spec, any_spec, any_spec, vm],
         out_specs=vm,
-        scratch_shapes=[pltpu.VMEM((28, BLK, HD), bf)] * (2 * nh)
+        scratch_shapes=[pltpu.VMEM((20, BLK, HD), bf)] * (2 * nh)
         + [pltpu.VMEM((16, BLK, HD), bf)] * nh
         + [pltpu.VMEM((4, 5, BLK, HD), bf)] * (2 * nh)
+        + [pltpu.VMEM((n, HD, width), bf) for n in (4, 4, 8)]
+        + [pltpu.VMEM((8 * rows, HD), bf)] * nh
+        + [pltpu.VMEM((2, rows, 4 * HD), bf)] * 2
+        + [pltpu.VMEM((rows, 8 * HD), bf)]
+        + [pltpu.VMEM((8, BLK, HD), bf)] * (2 * nh)
         + [
             pltpu.VMEM((4, 8, 128), jnp.int32),
             pltpu.SMEM((4, 8, 128), jnp.int32),
+            pltpu.VMEM((2 * rows, width), jnp.float32),
+            pltpu.VMEM((2 * rows, width), bf),
+            pltpu.VMEM((rows, width), bf),
             dma((9,)), dma((9,)),
             dma((36,)), dma((36,)),
             dma((9,)), dma((9,)),
             dma((12,)), dma((12,)),
             dma((8,)),
+            dma((29,)), dma((29,)),
+            dma((4,)), dma((7,)),
         ],
         compiler_params=pltpu.CompilerParams(
-            collective_id=0, has_side_effects=True, vmem_limit_bytes=48 << 20
+            collective_id=0, has_side_effects=True, vmem_limit_bytes=60 << 20
         ),
         name="attend",
-    )(query_tokens, key_tokens, value_tokens, lists)
-    return lax.psum_scatter(
-        jnp.dot(attended, out_weight, preferred_element_type=jnp.float32).astype(jnp.bfloat16),
-        "head",
-        scatter_dimension=0,
-        tiled=True,
-    )
+    )(query_tokens, key_tokens, value_tokens, out_weight, lists)
 
 
 def solution(mesh):

time: 182 us -> 103 us (0.57)
  waiting for transfers between devices: 82.8 us -> 0 us
  Pallas kernels: 78.2 us -> 98.7 us
  between operations: 13.4 us -> 0.01 us
  matrix products: 3.47 us -> 0 us
    reduce_scatter x1 -> x0, waiting for transfers between devices: 82.8 us -> none  [on_device(): lax.psum_scatter(jnp.dot(attended, out_weight, preferred_element_type=jnp...]
    pallas_call x1, Pallas kernels: 78.2 us -> 98.7 us  [on_device(): pl.pallas_call(kernel, out_shape=jax.ShapeDtypeStruct((rows, width), bf),...]
    dot_general x1 -> x0, matrix products: 3.47 us -> none  [on_device(): jnp.dot(attended, out_weight, preferred_element_type=jnp.float32)]
  transfers between devices with their start and end apart: 1 -> 0, of which waited for: 1 -> 0; matrix products, arithmetic and copies ran while one was open for 0% -> 0% of each run, Pallas kernels for 0% -> 0%
where the time goes in v2:
time: 103 us; the launch traced here: 102 us
  Pallas kernels  98.7 us (96%)
  local copies, waits for them, and re-layouts  3.04 us (3%)
    pallas_call x1, Pallas kernels, on_device(): pl.pallas_call(kernel, out_shape=jax.ShapeDtypeStruct((rows, width), bf),...  98.7 us

profile of v2, /device:TPU:8, one launch (start us, length us, event | category | flops | bytes accessed | tf_op | source)
XLA Modules:
  0.0 101.7 jit_solution(5473072299573339679)
XLA Ops:
  0.0 1.3 %pad.4.kvb_ref = s32[8,128]{1,0:T(8,128)} pad(s32[4,16]{1,0:T(4,128)} %param.9, s32[]{:T(128)} %constant.0.clone.1), padding=0_4x0_112 | pad | bytes 4356 | tf_op jit(solution)/shard_map/jit(_pad)/pad | solution.py:472
  1.3 98.7 %attend.1 = bf16[64,3072]{1,0:T(8,128)(2,1)} custom-call(bf16[64,3072]{1,0:T(8,128)(2,1)} %q_hbm.1, bf16[64,3072]{1,0:T(8,128)(2,1)} %k_hbm.1, bf16[64,3072]{1,0:T(8,128)(2,1)} %v_hbm.1, bf16[384,3072]{1,0:T(8,128)(2,1)} %w_hbm.1, s32[8,128]{1,0:T(8,128)} %pad.4.kvb_ref), custom_call_target="tpu_custom_call" | custom-call | tf_op jit(solution)/shard_map/attend/pallas_call | solution.py:477
  100.0 1.8 %copy.7 = bf16[64,3072]{1,0:T(8,128)(2,1)} copy(bf16[64,3072]{1,0:T(8,128)(2,1)} %attend.1) | data formatting | bytes 786432

commit v3 on v2

--- a/solution.py
+++ b/solution.py
@@ -11,35 +11,25 @@
 HD = 128
 BLK = 128
 HEADS_DEV = 3
+NAMES = ("unit", "merge", "proj", "qsend", "qfwd", "w1r", "w1", "w2r", "xor", "xo")
 MESH = pl.DeviceIdType.MESH
 ABSENT = -(2.0**100)
-SCALE = 1.0 / math.sqrt(HD)
+SCALE = math.log2(math.e) / math.sqrt(HD)
 
 OWN, M1, P1, M2, P2, MIR, TMP = range(7)
 UP = {1: M1, 2: M2, 3: TMP, 4: MIR}
 DOWN = {1: P1, 2: P2, 3: TMP, 4: MIR}
-ORDER = [
-    ("A", 0, 1), ("B", 0, 1), ("A", 0, 2), ("B", 0, 2), ("A", 1, 1), ("A", 0, 3),
-    ("B", 1, 1), ("A", 1, 2), ("A", 0, 4), ("B", 1, 2), ("A", 1, 3), ("A", 2, 1),
-    ("A", 1, 4), ("B", 2, 1), ("A", 2, 2), ("B", 2, 2), ("A", 2, 3), ("A", 2, 4),
-]
-WORK = {
-    0: ["a2a Q0", "a2a K1", "a2a V1"],
-    1: ["a2a K2", "a2a V2", "a2a Q1", "a2a Q2", "wown", "w1 2", "xo0"],
-    2: ["qsend 0"],
-    3: ["w1 0", "qfwd 0"],
-    6: ["unit 0 3", "unit 0 2", "qsend 1"],
-    7: ["unit 0 1", "qfwd 1"],
-    8: ["w1r 2", "w1 1"],
-    9: ["xor 0", "qsend 2"],
-    10: ["qfwd 2"],
-    11: ["unit 0 0", "merge 0", "w1r 0", "unit 1 3", "unit 1 2"],
-    12: ["unit 1 1", "w2r 2"],
-    14: ["w1r 1", "unit 1 0", "merge 1"],
-    15: ["w2r 0", "xor 1", "xor 2"],
-    16: ["unit 2 3", "unit 2 2", "xor 3"],
-    17: ["unit 2 1", "w2r 1", "proj 0", "proj 1", "unit 2 0", "merge 2", "final"],
-}
+HOPS = [(kind, h, hop) for h in range(HEADS_DEV) for kind, n in (("A", 4), ("B", 2)) for hop in range(1, n + 1)]
+JOBS = (
+    "a2aV0", "a2aK0", "a2aK1", "a2aV1", "a2aV2", "zUB01", "zDA01", "a2aQ2", "zUA01", "zDB01", "a2aQ0",
+    "zUA11", "zDB11", "a2aQ1", "zUB11", "zDA11", "a2aK2", "xo0", "w12", "w10", "qsend2", "zDA02", "zUB02",
+    "qsend0", "qsend1", "zUA02", "zDB02", "zUA12", "zDB12", "qfwd2", "zUB12", "zDA12", "qfwd0", "w11",
+    "zUA21", "zDA03", "qfwd1", "unit03", "zUA03", "zDA21", "unit02", "unit01", "zUB21", "zDB21", "xor0",
+    "unit13", "w1r2", "zDA13", "zUA13", "unit12", "unit11", "zDA04", "zUA22", "zUA04", "zDA22", "zUB22",
+    "zDB22", "w1r0", "zUA14", "zDA14", "w2r2", "zUA23", "w1r1", "unit00", "zDA23", "merge0", "w2r0",
+    "unit22", "xor1", "xor2", "unit23", "unit10", "merge1", "w2r1", "proj0", "zUA24", "zDA24", "unit21",
+    "proj1", "xor3", "unit20", "merge2", "final",
+)
 
 
 def kernel(q_hbm, k_hbm, v_hbm, w_hbm, kvb_ref, out_ref, *scratch):
@@ -121,11 +111,6 @@
         )
     kv_own = pltpu.make_async_copy(kvb_ref, kvb_all.at[r], misc.at[0])
 
-    for x, h in list(a2a_idx)[:2]:
-        a2a_start(x, h)
-    kv_own.start()
-    for cp in kv_copies:
-        cp.start()
 
     def tensor(direction, kind):
         return (kb, km) if (direction == "U") == (kind == "A") else (vb, vm)
@@ -135,32 +120,29 @@
 
     zname = {}
 
-    def zcopy(direction, n):
-        kind, h, hop = ORDER[n]
+    def zcopy(direction, kind, h, hop):
         slots = UP if direction == "U" else DOWN
         bufs = tensor(direction, kind)
         s_src = OWN if hop == 1 else slots[hop - 1]
         s_dst = slots[hop]
-        k = n + (len(ORDER) if direction == "D" else 0)
+        k = HOPS.index((kind, h, hop)) + (len(HOPS) if direction == "D" else 0)
         return pltpu.make_async_remote_copy(
             src_ref=slot_ref(bufs, h, s_src), dst_ref=slot_ref(bufs, h, s_dst),
             send_sem=zs.at[k], recv_sem=zr.at[k], device_id=zdev[direction], device_id_type=MESH,
         )
 
-    def z_wait(direction, n):
-        if ("z", direction, n) in done:
-            return
-        done.add(("z", direction, n))
-        zcopy(direction, n).wait_recv()
-
-    def z_step(direction, n):
-        kind, h, hop = ORDER[n]
+    def z_wait(*key):
+        if key not in done:
+            done.add(key)
+            zcopy(*key).wait_recv()
+
+    def z_step(direction, kind, h, hop):
         if hop == 1:
             is_k = (direction == "U") == (kind == "A")
             a2a_wait("K" if is_k else "V", h)
         else:
-            z_wait(direction, ORDER.index((kind, h, hop - 1)))
-        zcopy(direction, n).start()
+            z_wait(direction, kind, h, hop - 1)
+        zcopy(direction, kind, h, hop).start()
 
     def q_copy(h, i):
         ref = qb_[h].at[pl.ds(plane_r[2 if i == 3 else 0] * 4, 4)]
@@ -196,6 +178,7 @@
         cp.wait()
 
     lane = lax.broadcasted_iota(jnp.int32, (BLK, BLK), 1)
+    ones = jnp.ones((BLK, HD), jnp.bfloat16)
 
     def o_copy(h, i):
         return pltpu.make_async_remote_copy(
@@ -208,10 +191,10 @@
         q_wait(h)
         for x in "KV":
             a2a_wait(x, h)
-        for n, (_, hh, hop) in enumerate(ORDER):
+        for kind, hh, hop in HOPS:
             if hh == h and hop in ((1, 2, 4) if i == 0 else (1, 2)):
-                z_wait("U", n)
-                z_wait("D", n)
+                z_wait("U", kind, h, hop)
+                z_wait("D", kind, h, hop)
         rq = plane_r[i]
         dl = r - rq
         gt = lax.div(dl + 3, 4)
@@ -234,25 +217,22 @@
                 bias = jnp.where(e >= 0, 0.0, ABSENT).astype(jnp.float32)
                 s = lax.dot_general(q, keys[idx], (((1,), (1,)), ((), ())), preferred_element_type=jnp.float32)
                 scores.append(s * SCALE + bias)
-                vals.append(values[idx])
+                vals.append(jnp.concatenate([values[idx], ones], axis=1))
             top = functools.reduce(jnp.maximum, scores)
             m = jnp.max(top, axis=1, keepdims=True).astype(jnp.bfloat16).astype(jnp.float32)
-            ps = [jnp.exp(s - m) for s in scores]
-            l = jnp.sum(functools.reduce(jnp.add, ps), axis=1, keepdims=True)
+            ps = [jnp.exp2(s - m).astype(jnp.bfloat16) for s in scores]
             o = functools.reduce(
                 jnp.add,
-                [
-                    jnp.dot(p.astype(jnp.bfloat16), v, preferred_element_type=jnp.float32)
-                    for p, v in zip(ps, vals)
-                ],
+                [jnp.dot(p, v, preferred_element_type=jnp.float32) for p, v in zip(ps, vals)],
             )
-            os_[h][i, j] = o.astype(jnp.bfloat16)
+            os_[h][i, j] = o[:, :HD].astype(jnp.bfloat16)
+            l = o[:, HD:]
             l_hi = l.astype(jnp.bfloat16).astype(jnp.float32)
             stats = jnp.where(lane == j, m, stats)
             stats = jnp.where(lane == j + 4, l_hi, stats)
             return jnp.where(lane == j + 8, l - l_hi, stats)
 
-        stats = lax.fori_loop(0, 4, block, jnp.zeros((BLK, BLK), jnp.float32))
+        stats = lax.fori_loop(0, 4, block, jnp.zeros((BLK, BLK), jnp.float32), unroll=4)
         os_[h][i, 4] = stats.astype(jnp.bfloat16)
         if i:
             o_copy(h, i).start()
@@ -266,7 +246,7 @@
             ms = [s[:, j : j + 1] for s in stats]
             ls = [s[:, j + 4 : j + 5] + s[:, j + 8 : j + 9] for s in stats]
             top = functools.reduce(jnp.maximum, ms)
-            ws = [jnp.exp(m - top) for m in ms]
+            ws = [jnp.exp2(m - top) for m in ms]
             inv = 1.0 / functools.reduce(jnp.add, [w * l for w, l in zip(ws, ls)])
             o = functools.reduce(
                 jnp.add, [(w * inv) * bf[j].astype(jnp.float32) for w, bf in zip(ws, bufs)]
@@ -395,26 +375,27 @@
         lax.fori_loop(0, pacc.shape[1] // step, one, 0)
 
     def job(text):
-        name, *rest = text.split(" ")
-        if name == "a2a":
-            a2a_start(rest[0][0], int(rest[0][1]))
+        if text[:3] == "a2a":
+            a2a_start(text[3], int(text[4]))
             return
-        v = [int(a) for a in rest]
+        if text[0] == "z":
+            z_step(text[1], text[2], int(text[3]), int(text[4]))
+            return
+        if text == "final":
+            final()
+            return
+        name = next(a for a in NAMES if text.startswith(a))
+        v = [int(a) for a in text[len(name) :]]
         if name == "unit":
             unit(*v)
         elif name == "merge":
             merge(*v)
         elif name == "proj":
             project(*v)
-        elif name == "final":
-            final()
         elif name == "qsend":
             q_send(*v)
         elif name == "qfwd":
             q_fwd(*v)
-        elif name == "wown":
-            for h in range(nh):
-                w_own(h).start()
         elif name == "w1":
             go(w_hop1(v[0], 1))
             go(w_hop1(v[0], 3))
@@ -436,22 +417,26 @@
             go(w_sib(h, 2))
             if h == 2:
                 go(x_piece(2))
-        elif name == "xo0":
+        elif name == "xo":
             go(x_piece(0))
         elif name == "xor":
             k = (0, 1, 3, 2)[v[0]]
             x_piece(k).wait_recv()
             go(x_sib(k))
 
-    for n in range(len(ORDER)):
-        z_step("U", n)
-        z_step("D", n)
-        for text in WORK.get(n, ()):
-            job(text)
-
-    for n in range(len(ORDER)):
+    kv_own.start()
+    for cp in kv_copies:
+        cp.start()
+    for text in JOBS[:2]:
+        job(text)
+    for h in range(nh):
+        w_own(h).start()
+    for text in JOBS[2:]:
+        job(text)
+
+    for key in HOPS:
         for direction in "UD":
-            zcopy(direction, n).wait_send()
+            zcopy(direction, *key).wait_send()
     for h in range(nh):
         for i in (1, 2, 3):
             q_copy(h, i).wait_send()
@@ -469,7 +454,6 @@
 def on_device(query_tokens, key_tokens, value_tokens, out_weight, kv_blocks):
     nh = HEADS_DEV
     rows, width = query_tokens.shape
-    lists = jnp.pad(kv_blocks, ((0, 4), (0, 128 - kv_blocks.shape[1])), constant_values=-1)
     any_spec = pl.BlockSpec(memory_space=pl.ANY)
     vm = pl.BlockSpec(memory_space=pltpu.VMEM)
     bf = jnp.bfloat16
@@ -488,8 +472,8 @@
         + [pltpu.VMEM((rows, 8 * HD), bf)]
         + [pltpu.VMEM((8, BLK, HD), bf)] * (2 * nh)
         + [
-            pltpu.VMEM((4, 8, 128), jnp.int32),
-            pltpu.SMEM((4, 8, 128), jnp.int32),
+            pltpu.VMEM((4, *kv_blocks.shape), jnp.int32),
+            pltpu.SMEM((4, *kv_blocks.shape), jnp.int32),
             pltpu.VMEM((2 * rows, width), jnp.float32),
             pltpu.VMEM((2 * rows, width), bf),
             pltpu.VMEM((rows, width), bf),
@@ -505,7 +489,7 @@
             collective_id=0, has_side_effects=True, vmem_limit_bytes=60 << 20
         ),
         name="attend",
-    )(query_tokens, key_tokens, value_tokens, out_weight, lists)
+    )(query_tokens, key_tokens, value_tokens, out_weight, kv_blocks)
 
 
 def solution(mesh):

time: 103 us -> 88 us (0.85); the launches traced: 102 us -> 87.9 us
  Pallas kernels: 98.7 us -> 86.1 us
  local copies, waits for them, and re-layouts: 3.04 us -> 1.77 us
    pallas_call x1, Pallas kernels: 98.7 us -> 86.1 us  [on_device(): pl.pallas_call(kernel, out_shape=jax.ShapeDtypeStruct((rows, width), bf),...]
    pad x1 -> x0, local copies, waits for them, and re-layouts: 1.28 us -> none  [on_device(): jnp.pad(kv_blocks, ((0, 4), (0, 128 - kv_blocks.shape[1])), constant_valu...]
where the time goes in v3:
time: 88 us; the launch traced here: 87.9 us
  Pallas kernels  86.1 us (98%)
  local copies, waits for them, and re-layouts  1.77 us (2%)
    pallas_call x1, Pallas kernels, on_device(): pl.pallas_call(kernel, out_shape=jax.ShapeDtypeStruct((rows, width), bf),...  86.1 us
    unnamed x1, local copies, waits for them, and re-layouts  1.77 us

profile of v3, /device:TPU:8, one launch (start us, length us, event | category | flops | bytes accessed | tf_op | source)
XLA Modules:
  0.0 87.9 jit_solution(8368193879451747763)
XLA Ops:
  0.0 86.1 %attend.1 = bf16[64,3072]{1,0:T(8,128)(2,1)} custom-call(bf16[64,3072]{1,0:T(8,128)(2,1)} %q_hbm.1, bf16[64,3072]{1,0:T(8,128)(2,1)} %k_hbm.1, bf16[64,3072]{1,0:T(8,128)(2,1)} %v_hbm.1, bf16[384,3072]{1,0:T(8,128)(2,1)} %w_hbm.1, s32[4,16]{1,0:T(4,128)} %kvb_ref.1), custom_call_target="tpu_custom_call" | custom-call | tf_op jit(solution)/shard_map/attend/pallas_call | solution.py:461
  86.1 1.8 %copy.7 = bf16[64,3072]{1,0:T(8,128)(2,1)} copy(bf16[64,3072]{1,0:T(8,128)(2,1)} %attend.1) | data formatting | bytes 786432

commit v4 on v3

--- a/solution.py
+++ b/solution.py
@@ -21,21 +21,21 @@
 DOWN = {1: P1, 2: P2, 3: TMP, 4: MIR}
 HOPS = [(kind, h, hop) for h in range(HEADS_DEV) for kind, n in (("A", 4), ("B", 2)) for hop in range(1, n + 1)]
 JOBS = (
-    "a2aV0", "a2aK0", "a2aK1", "a2aV1", "a2aV2", "zUB01", "zDA01", "a2aQ2", "zUA01", "zDB01", "a2aQ0",
-    "zUA11", "zDB11", "a2aQ1", "zUB11", "zDA11", "a2aK2", "xo0", "w12", "w10", "qsend2", "zDA02", "zUB02",
-    "qsend0", "qsend1", "zUA02", "zDB02", "zUA12", "zDB12", "qfwd2", "zUB12", "zDA12", "qfwd0", "w11",
-    "zUA21", "zDA03", "qfwd1", "unit03", "zUA03", "zDA21", "unit02", "unit01", "zUB21", "zDB21", "xor0",
-    "unit13", "w1r2", "zDA13", "zUA13", "unit12", "unit11", "zDA04", "zUA22", "zUA04", "zDA22", "zUB22",
-    "zDB22", "w1r0", "zUA14", "zDA14", "w2r2", "zUA23", "w1r1", "unit00", "zDA23", "merge0", "w2r0",
-    "unit22", "xor1", "xor2", "unit23", "unit10", "merge1", "w2r1", "proj0", "zUA24", "zDA24", "unit21",
-    "proj1", "xor3", "unit20", "merge2", "final",
+    "a2aK0", "a2aV0", "a2aV1", "a2aK1", "a2aQ0", "zUA01", "zDB01", "a2aQ2", "zUB01", "zDA01", "a2aQ1",
+    "zUB11", "zDA11", "a2aV2", "zUA11", "zDB11", "a2aK2", "w11", "w12", "xo0", "qsend0", "zUA02", "zDB02",
+    "qsend2", "qsend1", "zUB02", "zDA02", "zUB21", "zDA21", "zDB21", "zUA21", "zDA12", "zUB12", "zDB12",
+    "qfwd0", "zUA12", "qfwd2", "w10", "zUA03", "qfwd1", "zDA03", "unit02", "unit01", "unit03", "zDA22",
+    "zUB22", "xor0", "zUA22", "zDB22", "w1r1", "w1r2", "zDA13", "zUA13", "unit11", "unit13", "unit12",
+    "zDA04", "zUA04", "zDA23", "zUA23", "unit22", "unit23", "w1r0", "zUA14", "zDA14", "unit21", "w2r1",
+    "w2r2", "unit00", "merge0", "xor1", "xor2", "zUA24", "zDA24", "w2r0", "unit10", "merge1", "proj0",
+    "unit20", "merge2", "xor3", "proj1", "proj2", "final",
 )
 
 
 def kernel(q_hbm, k_hbm, v_hbm, w_hbm, kvb_ref, out_ref, *scratch):
     nh = HEADS_DEV
     kb, vb, qb_, os_, or_, wb, att, ab, km, vm = (scratch[i * nh : (i + 1) * nh] for i in range(10))
-    (kvb_all, kvb_smem, pacc, pb, prec, a_send, a_recv, zs, zr, qs, qr, osem, orsem, misc, ws, wr, ts, tr) = scratch[10 * nh :]
+    (kvb_all, kvb_smem, pacc, pb, prec, obuf, a_send, a_recv, zs, zr, qs, qr, osem, orsem, misc, ws, wr, ts, tr) = scratch[10 * nh :]
     b = lax.axis_index("blk")
     g = lax.axis_index("head")
     z, r = lax.div(b, 4), lax.rem(b, 4)
@@ -331,15 +331,18 @@
             for k in range(4):
                 wait_bytes(wb[2].at[widx(2, k, True), :, ocol], wr.at[25 + k])
 
-    step = 512
+    step = 768
 
     def columns(t):
         return pl.ds(pl.multiple_of(t * step, step), step)
 
-    def project(h):
-        w_ready(h)
-        wait_bytes(ab[h], tr.at[h])
+    def project(k):
+        h = min(k, 1)
+        if k < 2:
+            w_ready(h)
+            wait_bytes(ab[h], tr.at[h])
         rows = ab[h][...].reshape(2 * 64, 4 * HD)
+        n = pacc.shape[1] // step
 
         def one(t, carry):
             col = columns(t)
@@ -350,29 +353,34 @@
             pacc[:, col] = res
             return carry
 
-        lax.fori_loop(0, pacc.shape[1] // step, one, 0)
+        lax.fori_loop(*((0, n), (0, n // 2), (n // 2, n))[k], one, 0)
         if h:
-            p_copy.start()
-
-    p_copy = pltpu.make_async_remote_copy(
-        src_ref=pb.at[pl.ds(pl.multiple_of((1 - xh) * 64, 64), 64), :], dst_ref=prec,
-        send_sem=ts.at[3], recv_sem=tr.at[6], device_id=xh_dev, device_id_type=MESH,
-    )
+            p_copy(k - 1).start()
+
+    def p_copy(k):
+        n = pb.shape[1] // 2
+        return pltpu.make_async_remote_copy(
+            src_ref=pb.at[pl.ds(pl.multiple_of((1 - xh) * 64, 64), 64), k * n : (k + 1) * n],
+            dst_ref=prec.at[:, k * n : (k + 1) * n],
+            send_sem=ts.at[3 + k], recv_sem=tr.at[6 + k], device_id=xh_dev, device_id_type=MESH,
+        )
+
+    def out_copy(t):
+        return pltpu.make_async_copy(obuf.at[:, columns(t)], out_ref.at[:, columns(t)], ts.at[5 + t])
 
     def final():
         w_ready(2)
         wait_bytes(ab[2], tr.at[2])
-        p_copy.wait_recv()
         rows = ab[2][...]
-
-        def one(t, carry):
-            col = columns(t)
+        n = pacc.shape[1] // step
+        for t in range(n):
+            if t % (n // 2) == 0:
+                p_copy(t // (n // 2)).wait_recv()
+            col = slice(t * step, (t + 1) * step)
             res = jnp.dot(rows, wb[2][:, :, col].reshape(8 * HD, step), preferred_element_type=jnp.float32)
             mine = pacc[pl.ds(pl.multiple_of(xh * 64, 64), 64), col]
-            out_ref[:, col] = (res + mine + prec[:, col].astype(jnp.float32)).astype(jnp.bfloat16)
-            return carry
-
-        lax.fori_loop(0, pacc.shape[1] // step, one, 0)
+            obuf[:, col] = (res + mine + prec[:, col].astype(jnp.float32)).astype(jnp.bfloat16)
+            out_copy(t).start()
 
     def job(text):
         if text[:3] == "a2a":
@@ -448,7 +456,10 @@
     wait_bytes(att[0].at[pl.ds(0, 6 * 64)], ts.at[0])
     wait_bytes(att[1].at[pl.ds(0, 6 * 64)], ts.at[1])
     wait_bytes(att[2].at[pl.ds(0, 7 * 64)], ts.at[2])
-    p_copy.wait_send()
+    for k in range(2):
+        p_copy(k).wait_send()
+    for t in range(pacc.shape[1] // step):
+        out_copy(t).wait()
 
 
 def on_device(query_tokens, key_tokens, value_tokens, out_weight, kv_blocks):
@@ -462,7 +473,7 @@
         kernel,
         out_shape=jax.ShapeDtypeStruct((rows, width), bf),
         in_specs=[any_spec, any_spec, any_spec, any_spec, vm],
-        out_specs=vm,
+        out_specs=any_spec,
         scratch_shapes=[pltpu.VMEM((20, BLK, HD), bf)] * (2 * nh)
         + [pltpu.VMEM((16, BLK, HD), bf)] * nh
         + [pltpu.VMEM((4, 5, BLK, HD), bf)] * (2 * nh)
@@ -477,13 +488,14 @@
             pltpu.VMEM((2 * rows, width), jnp.float32),
             pltpu.VMEM((2 * rows, width), bf),
             pltpu.VMEM((rows, width), bf),
+            pltpu.VMEM((rows, width), bf),
             dma((9,)), dma((9,)),
             dma((36,)), dma((36,)),
             dma((9,)), dma((9,)),
             dma((12,)), dma((12,)),
             dma((8,)),
             dma((29,)), dma((29,)),
-            dma((4,)), dma((7,)),
+            dma((9,)), dma((8,)),
         ],
         compiler_params=pltpu.CompilerParams(
             collective_id=0, has_side_effects=True, vmem_limit_bytes=60 << 20

time: 88 us -> 85.5 us (0.972)
  Pallas kernels: 86.1 us -> 83 us
    pallas_call x1, Pallas kernels: 86.1 us -> 83 us  [on_device(): pl.pallas_call(kernel, out_shape=jax.ShapeDtypeStruct((rows, width), bf),...]
where the time goes in v4:
time: 85.5 us; the launch traced here: 84.8 us
  Pallas kernels  83 us (97%)
  local copies, waits for them, and re-layouts  1.77 us (2%)
    pallas_call x1, Pallas kernels, on_device(): pl.pallas_call(kernel, out_shape=jax.ShapeDtypeStruct((rows, width), bf),...  83 us
    unnamed x1, local copies, waits for them, and re-layouts  1.77 us

profile of v4, /device:TPU:8, one launch (start us, length us, event | category | flops | bytes accessed | tf_op | source)
XLA Modules:
  0.0 84.8 jit_solution(1610435825261051629)
XLA Ops:
  0.0 83.0 %attend.1 = bf16[64,3072]{1,0:T(8,128)(2,1)} custom-call(bf16[64,3072]{1,0:T(8,128)(2,1)} %q_hbm.1, bf16[64,3072]{1,0:T(8,128)(2,1)} %k_hbm.1, bf16[64,3072]{1,0:T(8,128)(2,1)} %v_hbm.1, bf16[384,3072]{1,0:T(8,128)(2,1)} %w_hbm.1, s32[4,16]{1,0:T(4,128)} %kvb_ref.1), custom_call_target="tpu_custom_call" | custom-call | tf_op jit(solution)/shard_map/attend/pallas_call | solution.py:472
  83.0 1.8 %copy.7 = bf16[64,3072]{1,0:T(8,128)(2,1)} copy(bf16[64,3072]{1,0:T(8,128)(2,1)} %attend.1) | data formatting | bytes 786432

commit v5 on v4

--- a/solution.py
+++ b/solution.py
@@ -21,21 +21,21 @@
 DOWN = {1: P1, 2: P2, 3: TMP, 4: MIR}
 HOPS = [(kind, h, hop) for h in range(HEADS_DEV) for kind, n in (("A", 4), ("B", 2)) for hop in range(1, n + 1)]
 JOBS = (
-    "a2aK0", "a2aV0", "a2aV1", "a2aK1", "a2aQ0", "zUA01", "zDB01", "a2aQ2", "zUB01", "zDA01", "a2aQ1",
-    "zUB11", "zDA11", "a2aV2", "zUA11", "zDB11", "a2aK2", "w11", "w12", "xo0", "qsend0", "zUA02", "zDB02",
-    "qsend2", "qsend1", "zUB02", "zDA02", "zUB21", "zDA21", "zDB21", "zUA21", "zDA12", "zUB12", "zDB12",
-    "qfwd0", "zUA12", "qfwd2", "w10", "zUA03", "qfwd1", "zDA03", "unit02", "unit01", "unit03", "zDA22",
-    "zUB22", "xor0", "zUA22", "zDB22", "w1r1", "w1r2", "zDA13", "zUA13", "unit11", "unit13", "unit12",
-    "zDA04", "zUA04", "zDA23", "zUA23", "unit22", "unit23", "w1r0", "zUA14", "zDA14", "unit21", "w2r1",
-    "w2r2", "unit00", "merge0", "xor1", "xor2", "zUA24", "zDA24", "w2r0", "unit10", "merge1", "proj0",
-    "unit20", "merge2", "xor3", "proj1", "proj2", "final",
+    "a2aK0", "a2aK1", "a2aV0", "a2aV1", "a2aK2", "a2aQ2", "a2aQ1", "a2aQ0", "a2aV2", "w12", "xo0", "w10",
+    "w11", "zUA01", "zDB01", "zUA11", "zDB11", "zUB01", "zDA01", "zUB11", "zDA11", "zUA21", "zDB21", "zUA02",
+    "qsend2", "zDB02", "qsend1", "zUA12", "qsend0", "zDB12", "zUB21", "zUB02", "zDA21", "qfwd2", "zUB12",
+    "zDA02", "qfwd1", "zUA22", "zDB22", "xor0", "qfwd0", "zUA03", "zDA12", "zUA13", "zDA22", "w1r2", "zUB22",
+    "w1r0", "unit03", "unit02", "unit01", "zDA03", "zUA23", "zDA13", "unit13", "unit11", "zDA23", "zUA04",
+    "w2r2", "unit12", "zUA14", "zDA04", "w1r1", "zDA14", "unit22", "w2r0", "unit21", "xor1", "unit23",
+    "zUA24", "xor2", "zDA24", "unit00", "w2r1", "merge0", "unit10", "merge1", "unit20", "merge2", "xor3",
+    "proj0", "proj1", "proj2", "fin", "final",
 )
 
 
 def kernel(q_hbm, k_hbm, v_hbm, w_hbm, kvb_ref, out_ref, *scratch):
     nh = HEADS_DEV
     kb, vb, qb_, os_, or_, wb, att, ab, km, vm = (scratch[i * nh : (i + 1) * nh] for i in range(10))
-    (kvb_all, kvb_smem, pacc, pb, prec, obuf, a_send, a_recv, zs, zr, qs, qr, osem, orsem, misc, ws, wr, ts, tr) = scratch[10 * nh :]
+    (kvb_all, kvb_smem, pacc, pb, prec, obuf, total, a_send, a_recv, zs, zr, qs, qr, osem, orsem, misc, ws, wr, ts, tr) = scratch[10 * nh :]
     b = lax.axis_index("blk")
     g = lax.axis_index("head")
     z, r = lax.div(b, 4), lax.rem(b, 4)
@@ -333,9 +333,6 @@
 
     step = 768
 
-    def columns(t):
-        return pl.ds(pl.multiple_of(t * step, step), step)
-
     def project(k):
         h = min(k, 1)
         if k < 2:
@@ -344,42 +341,41 @@
         rows = ab[h][...].reshape(2 * 64, 4 * HD)
         n = pacc.shape[1] // step
 
-        def one(t, carry):
-            col = columns(t)
+        for t in range(*((0, n), (0, n // 2), (n // 2, n))[k]):
+            col = slice(t * step, (t + 1) * step)
             res = jnp.dot(rows, wb[h][:, :, col].reshape(4 * HD, step), preferred_element_type=jnp.float32)
             if h:
                 res = res + pacc[:, col]
                 pb[:, col] = res.astype(jnp.bfloat16)
+                p_copy(t).start()
             pacc[:, col] = res
-            return carry
-
-        lax.fori_loop(*((0, n), (0, n // 2), (n // 2, n))[k], one, 0)
-        if h:
-            p_copy(k - 1).start()
 
     def p_copy(k):
-        n = pb.shape[1] // 2
         return pltpu.make_async_remote_copy(
-            src_ref=pb.at[pl.ds(pl.multiple_of((1 - xh) * 64, 64), 64), k * n : (k + 1) * n],
-            dst_ref=prec.at[:, k * n : (k + 1) * n],
+            src_ref=pb.at[pl.ds(pl.multiple_of((1 - xh) * 64, 64), 64), k * step : (k + 1) * step],
+            dst_ref=prec.at[:, k * step : (k + 1) * step],
             send_sem=ts.at[3 + k], recv_sem=tr.at[6 + k], device_id=xh_dev, device_id_type=MESH,
         )
 
     def out_copy(t):
-        return pltpu.make_async_copy(obuf.at[:, columns(t)], out_ref.at[:, columns(t)], ts.at[5 + t])
-
-    def final():
+        return pltpu.make_async_copy(obuf.at[:, t * step : (t + 1) * step], out_ref.at[:, t * step : (t + 1) * step], ts.at[7 + t])
+
+    mine = pl.ds(pl.multiple_of(xh * 64, 64), 64)
+
+    def last_head():
         w_ready(2)
         wait_bytes(ab[2], tr.at[2])
         rows = ab[2][...]
-        n = pacc.shape[1] // step
-        for t in range(n):
-            if t % (n // 2) == 0:
-                p_copy(t // (n // 2)).wait_recv()
+        for t in range(pacc.shape[1] // step):
             col = slice(t * step, (t + 1) * step)
             res = jnp.dot(rows, wb[2][:, :, col].reshape(8 * HD, step), preferred_element_type=jnp.float32)
-            mine = pacc[pl.ds(pl.multiple_of(xh * 64, 64), 64), col]
-            obuf[:, col] = (res + mine + prec[:, col].astype(jnp.float32)).astype(jnp.bfloat16)
+            total[:, col] = res + pacc[mine, col]
+
+    def final():
+        for t in range(pacc.shape[1] // step):
+            p_copy(t).wait_recv()
+            col = slice(t * step, (t + 1) * step)
+            obuf[:, col] = (total[:, col] + prec[:, col].astype(jnp.float32)).astype(jnp.bfloat16)
             out_copy(t).start()
 
     def job(text):
@@ -389,8 +385,8 @@
         if text[0] == "z":
             z_step(text[1], text[2], int(text[3]), int(text[4]))
             return
-        if text == "final":
-            final()
+        if text in ("fin", "final"):
+            (last_head if text == "fin" else final)()
             return
         name = next(a for a in NAMES if text.startswith(a))
         v = [int(a) for a in text[len(name) :]]
@@ -456,9 +452,8 @@
     wait_bytes(att[0].at[pl.ds(0, 6 * 64)], ts.at[0])
     wait_bytes(att[1].at[pl.ds(0, 6 * 64)], ts.at[1])
     wait_bytes(att[2].at[pl.ds(0, 7 * 64)], ts.at[2])
-    for k in range(2):
-        p_copy(k).wait_send()
     for t in range(pacc.shape[1] // step):
+        p_copy(t).wait_send()
         out_copy(t).wait()
 
 
@@ -489,13 +484,14 @@
             pltpu.VMEM((2 * rows, width), bf),
             pltpu.VMEM((rows, width), bf),
             pltpu.VMEM((rows, width), bf),
+            pltpu.VMEM((rows, width), jnp.float32),
             dma((9,)), dma((9,)),
             dma((36,)), dma((36,)),
             dma((9,)), dma((9,)),
             dma((12,)), dma((12,)),
             dma((8,)),
             dma((29,)), dma((29,)),
-            dma((9,)), dma((8,)),
+            dma((11,)), dma((10,)),
         ],
         compiler_params=pltpu.CompilerParams(
             collective_id=0, has_side_effects=True, vmem_limit_bytes=60 << 20

time: 85.5 us -> 83.6 us (0.978)
  Pallas kernels: 83 us -> 81.6 us
    pallas_call x1, Pallas kernels: 83 us -> 81.6 us  [on_device(): pl.pallas_call(kernel, out_shape=jax.ShapeDtypeStruct((rows, width), bf),...]
where the time goes in v5:
time: 83.6 us; the launch traced here: 83.4 us
  Pallas kernels  81.6 us (98%)
  local copies, waits for them, and re-layouts  1.77 us (2%)
    pallas_call x1, Pallas kernels, on_device(): pl.pallas_call(kernel, out_shape=jax.ShapeDtypeStruct((rows, width), bf),...  81.6 us
    unnamed x1, local copies, waits for them, and re-layouts  1.77 us

profile of v5, /device:TPU:8, one launch (start us, length us, event | category | flops | bytes accessed | tf_op | source)
XLA Modules:
  0.0 83.4 jit_solution(13979082204514951494)
XLA Ops:
  0.0 81.6 %attend.1 = bf16[64,3072]{1,0:T(8,128)(2,1)} custom-call(bf16[64,3072]{1,0:T(8,128)(2,1)} %q_hbm.1, bf16[64,3072]{1,0:T(8,128)(2,1)} %k_hbm.1, bf16[64,3072]{1,0:T(8,128)(2,1)} %v_hbm.1, bf16[384,3072]{1,0:T(8,128)(2,1)} %w_hbm.1, s32[4,16]{1,0:T(4,128)} %kvb_ref.1), custom_call_target="tpu_custom_call" | custom-call | tf_op jit(solution)/shard_map/attend/pallas_call | solution.py:467
  81.6 1.8 %copy.7 = bf16[64,3072]{1,0:T(8,128)(2,1)} copy(bf16[64,3072]{1,0:T(8,128)(2,1)} %attend.1) | data formatting | bytes 786432

commit v6 on v5

--- a/solution.py
+++ b/solution.py
@@ -21,21 +21,21 @@
 DOWN = {1: P1, 2: P2, 3: TMP, 4: MIR}
 HOPS = [(kind, h, hop) for h in range(HEADS_DEV) for kind, n in (("A", 4), ("B", 2)) for hop in range(1, n + 1)]
 JOBS = (
-    "a2aK0", "a2aK1", "a2aV0", "a2aV1", "a2aK2", "a2aQ2", "a2aQ1", "a2aQ0", "a2aV2", "w12", "xo0", "w10",
-    "w11", "zUA01", "zDB01", "zUA11", "zDB11", "zUB01", "zDA01", "zUB11", "zDA11", "zUA21", "zDB21", "zUA02",
-    "qsend2", "zDB02", "qsend1", "zUA12", "qsend0", "zDB12", "zUB21", "zUB02", "zDA21", "qfwd2", "zUB12",
-    "zDA02", "qfwd1", "zUA22", "zDB22", "xor0", "qfwd0", "zUA03", "zDA12", "zUA13", "zDA22", "w1r2", "zUB22",
-    "w1r0", "unit03", "unit02", "unit01", "zDA03", "zUA23", "zDA13", "unit13", "unit11", "zDA23", "zUA04",
-    "w2r2", "unit12", "zUA14", "zDA04", "w1r1", "zDA14", "unit22", "w2r0", "unit21", "xor1", "unit23",
-    "zUA24", "xor2", "zDA24", "unit00", "w2r1", "merge0", "unit10", "merge1", "unit20", "merge2", "xor3",
-    "proj0", "proj1", "proj2", "fin", "final",
+    "a2aK0", "a2aV0", "a2aV1", "a2aK1", "a2aQ0", "a2aQ1", "a2aK2", "a2aV2", "a2aQ2", "w10", "w12", "xo0",
+    "zDB01", "zUA01", "zDA01", "zUB01", "zDA11", "zUB11", "zUA11", "zDB11", "qsend0", "zDB02", "zUA02",
+    "qsend1", "zUA21", "zDB21", "zDA02", "zUB02", "zUB21", "zDA21", "qsend2", "zDA12", "zUB12", "zDB12",
+    "zUA12", "qfwd0", "qfwd1", "w11", "zUA03", "qfwd2", "zDB22", "zUA22", "zDA03", "unit03", "unit02",
+    "xor0", "zDA22", "zUB22", "unit01", "w1r0", "zDA13", "w1r2", "zUA13", "unit12", "unit13", "unit11",
+    "zUA04", "zDA04", "zUA23", "zDA23", "unit22", "w2r0", "unit23", "w1r1", "zDA14", "zUA14", "unit21",
+    "w2r2", "unit00", "merge0", "xor1", "xor2", "zDA24", "zUA24", "w2r1", "unit10", "merge1", "proj0",
+    "unit20", "merge2", "proj1", "proj2", "xor3", "fin", "final",
 )
 
 
-def kernel(q_hbm, k_hbm, v_hbm, w_hbm, kvb_ref, out_ref, *scratch):
+def kernel(q_hbm, k_hbm, v_hbm, w_hbm, kvb_ref, out_ref, prec, *scratch):
     nh = HEADS_DEV
     kb, vb, qb_, os_, or_, wb, att, ab, km, vm = (scratch[i * nh : (i + 1) * nh] for i in range(10))
-    (kvb_all, kvb_smem, pacc, pb, prec, obuf, total, a_send, a_recv, zs, zr, qs, qr, osem, orsem, misc, ws, wr, ts, tr) = scratch[10 * nh :]
+    (kvb_all, kvb_smem, pacc, pb, total, a_send, a_recv, zs, zr, qs, qr, osem, orsem, misc, ws, wr, ts, tr) = scratch[10 * nh :]
     b = lax.axis_index("blk")
     g = lax.axis_index("head")
     z, r = lax.div(b, 4), lax.rem(b, 4)
@@ -358,7 +358,7 @@
         )
 
     def out_copy(t):
-        return pltpu.make_async_copy(obuf.at[:, t * step : (t + 1) * step], out_ref.at[:, t * step : (t + 1) * step], ts.at[7 + t])
+        return pltpu.make_async_copy(total.at[:, t * step : (t + 1) * step], out_ref.at[:, t * step : (t + 1) * step], ts.at[7 + t])
 
     mine = pl.ds(pl.multiple_of(xh * 64, 64), 64)
 
@@ -370,13 +370,11 @@
             col = slice(t * step, (t + 1) * step)
             res = jnp.dot(rows, wb[2][:, :, col].reshape(8 * HD, step), preferred_element_type=jnp.float32)
             total[:, col] = res + pacc[mine, col]
+            out_copy(t).start()
 
     def final():
         for t in range(pacc.shape[1] // step):
             p_copy(t).wait_recv()
-            col = slice(t * step, (t + 1) * step)
-            obuf[:, col] = (total[:, col] + prec[:, col].astype(jnp.float32)).astype(jnp.bfloat16)
-            out_copy(t).start()
 
     def job(text):
         if text[:3] == "a2a":
@@ -464,11 +462,11 @@
     vm = pl.BlockSpec(memory_space=pltpu.VMEM)
     bf = jnp.bfloat16
     dma = pltpu.SemaphoreType.DMA
-    return pl.pallas_call(
+    total, other = pl.pallas_call(
         kernel,
-        out_shape=jax.ShapeDtypeStruct((rows, width), bf),
+        out_shape=(jax.ShapeDtypeStruct((rows, width), jnp.float32), jax.ShapeDtypeStruct((rows, width), bf)),
         in_specs=[any_spec, any_spec, any_spec, any_spec, vm],
-        out_specs=any_spec,
+        out_specs=(any_spec, any_spec),
         scratch_shapes=[pltpu.VMEM((20, BLK, HD), bf)] * (2 * nh)
         + [pltpu.VMEM((16, BLK, HD), bf)] * nh
         + [pltpu.VMEM((4, 5, BLK, HD), bf)] * (2 * nh)
@@ -482,8 +480,6 @@
             pltpu.SMEM((4, *kv_blocks.shape), jnp.int32),
             pltpu.VMEM((2 * rows, width), jnp.float32),
             pltpu.VMEM((2 * rows, width), bf),
-            pltpu.VMEM((rows, width), bf),
-            pltpu.VMEM((rows, width), bf),
             pltpu.VMEM((rows, width), jnp.float32),
             dma((9,)), dma((9,)),
             dma((36,)), dma((36,)),
@@ -498,6 +494,7 @@
         ),
         name="attend",
     )(query_tokens, key_tokens, value_tokens, out_weight, kv_blocks)
+    return (total + other.astype(jnp.float32)).astype(bf)
 
 
 def solution(mesh):

time: 83.6 us -> 83.7 us (level)
  other arithmetic: 0 us -> 2.05 us
  local copies, waits for them, and re-layouts: 1.77 us -> 0 us
    convert_element_type x0 -> x1, other arithmetic: none -> 2.05 us  [on_device(): return (total + other.astype(jnp.float32)).astype(bf)]
    unnamed x1 -> x0, local copies, waits for them, and re-layouts: 1.77 us -> none
where the time goes in v6:
time: 83.7 us; the launch traced here: 83.6 us
  Pallas kernels  81.5 us (97%)
  other arithmetic  2.05 us (2%)
    pallas_call x1, Pallas kernels, on_device(): pl.pallas_call(kernel, out_shape=(jax.ShapeDtypeStruct((rows, width), jnp...  81.5 us
    convert_element_type x1, other arithmetic, on_device(): return (total + other.astype(jnp.float32)).astype(bf)  2.05 us

profile of v6, /device:TPU:8, one launch (start us, length us, event | category | flops | bytes accessed | tf_op | source)
XLA Modules:
  0.0 83.6 jit_solution(10844225542865398001)
XLA Ops:
  0.0 81.5 %attend.1 = (f32[64,3072]{1,0:T(8,128)}, bf16[64,3072]{1,0:T(8,128)(2,1)}) custom-call(bf16[64,3072]{1,0:T(8,128)(2,1)} %q_hbm.1, bf16[64,3072]{1,0:T(8,128)(2,1)} %k_hbm.1, bf16[64,3072]{1,0:T(8,128)(2,1)} %v_hbm.1, bf16[384,3072]{1,0:T(8,128)(2,1)} %w_hbm.1, s32[4,16]{1,0:T(4,128)} %kvb_ref.1), custom_call_target="tpu_custom_call" | custom-call | tf_op jit(solution)/shard_map/attend/pallas_call | solution.py:465
  81.5 2.0 %add_convert_fusion = bf16[64,3072]{1,0:T(8,128)(2,1)} fusion(f32[64,3072]{1,0:T(8,128)} %get-tuple-element.7, bf16[64,3072]{1,0:T(8,128)(2,1)} %get-tuple-element.8), kind=kLoop, calls=%fused_computation | loop fusion | flops 589824 | bytes 1572864 | tf_op jit(solution)/shard_map/convert_element_type | solution.py:497
